TPU v7x, 128 devices: a whole 4x4x4 slice. The times are simulated.
128 devices in a mesh: grp: 8 (over x, core), sub: 16 (over z, y).
Axes of the slice: x: 4, y: 4, z: 4, core: 2. Of those that a mesh axis runs over, the one named last changes fastest.
Arguments:
- points: bfloat16 [131072, 1024], P(('grp', 'sub')), may hold values from -16 to 16
- level1_ids: int32 [131072], P(('grp', 'sub')), may hold values from 0 to 1023
- level2_ids: int32 [131072], P(('grp', 'sub')), may hold values from 0 to 8191, as said below
- level3_ids: int32 [131072], P(('grp', 'sub')), may hold values from 0 to 255
- needed: int32 [128, 128], P(('grp', 'sub')), may hold values from 0 to 32767, as said below
- centroids1: bfloat16 [262144, 1024], P(('grp', 'sub')), may hold values from -6 to 6
- centroids2: bfloat16 [8, 8192, 1024], P('grp', 'sub'), may hold values from -3 to 3
- centroids3: bfloat16 [256, 1024], replicated, may hold values from -6 to 6
Outputs:
- level1_new: float32 [262144, 1024], P(('grp', 'sub'))
- level2_new: float32 [8, 8192, 1024], P('grp', 'sub')
- level3_new: float32 [256, 1024], replicated
Inputs may be any that keep to these rules, and one draw needn't show every extreme that they name: `needed`: each row lists distinct blocks; a row names at most 2 blocks held by one device (blocks of device o are o * 256 to o * 256 + 255), and names exactly 2 of some device's blocks. `level2_ids`: of one device's points, at most 128 have level-2 ids in any one range r * 8192 // 16 to (r + 1) * 8192 // 16 - 1, and exactly 128 in some range.
All inputs are finite; a program needn't handle non-finite values.
Results may differ from a plain program's by a relative error of at most 0.0055.
Values may be sent and summed in bfloat16 or wider, within the bound.
No kernel may reach another device: no remote copies, remote signals or barrier semaphores. Data moves between devices by JAX's collectives and lax.ppermute only.
A program may use at most 128 MiB of HBM per device.

v0:
```python
import jax
import jax.numpy as jnp
from jax import lax
from jax.sharding import PartitionSpec as P

D = 1024
K1_DEV = 2048
BLK = 8
CAP = 2
K2 = 8192
K3 = 256


def weighted_hot(labels, count, weights_low):
    return jnp.where(
        labels[:, None] == jnp.arange(count)[None, :],
        weights_low[:, None],
        jnp.zeros((), jnp.bfloat16),
    )


def column_sums(hot_table, points):
    return lax.dot_general(
        hot_table, points, (((0,), (0,)), ((), ())), preferred_element_type=jnp.float32
    )


def shards(points, level1_ids, level2_ids, level3_ids, needed, centroids1, centroids2, centroids3):
    devices = lax.axis_size(("grp", "sub"))
    sub_count = lax.axis_size("sub")
    blocks_dev = K1_DEV // BLK
    wanted = needed[0]
    owners = wanted // blocks_dev
    owner_hits = (owners[:, None] == jnp.arange(devices)[None, :]).astype(jnp.int32)
    places = jnp.sum(jnp.cumsum(owner_hits, axis=0) * owner_hits, axis=1) - 1
    slot_index = owners * CAP + places
    requests = jnp.zeros((devices * CAP,), jnp.int32).at[slot_index].set(wanted % blocks_dev)
    block_table = centroids1.reshape(blocks_dev, BLK * D)
    flat_asked = lax.all_to_all(
        requests.reshape(devices, 1, CAP), ("grp", "sub"), split_axis=0, concat_axis=0, tiled=True
    )[:, 0, :]
    served = lax.all_to_all(
        block_table[flat_asked], ("grp", "sub"), split_axis=0, concat_axis=0, tiled=True
    )
    fetched_rows = served.reshape(devices * CAP * BLK, D)
    matches = (level1_ids[:, None] // BLK == jnp.arange(wanted.shape[0])[None, :]).astype(jnp.int32)
    point_slots = jnp.sum(matches * slot_index[None, :], axis=1)
    row_index = point_slots * BLK + level1_ids % BLK
    nearest = fetched_rows[row_index].astype(jnp.float32)
    values = points.astype(jnp.float32)
    spread = jnp.sum((values - nearest) ** 2, axis=1) / D
    weights_low = (1.0 / (1.0 + spread)).astype(jnp.bfloat16)
    hot_one = weighted_hot(row_index, devices * CAP * BLK, weights_low)
    sums_one = column_sums(hot_one, points)
    mass_one = jnp.sum(hot_one.astype(jnp.float32), axis=0)
    back_sums, back_mass = (
        lax.all_to_all(
            sums_one.reshape(devices, CAP * BLK, D),
            ("grp", "sub"),
            split_axis=0,
            concat_axis=0,
            tiled=True,
        ),
        lax.all_to_all(
            mass_one.reshape(devices, CAP * BLK),
            ("grp", "sub"),
            split_axis=0,
            concat_axis=0,
            tiled=True,
        ),
    )
    owner_hot = (flat_asked.reshape(1, devices * CAP) == jnp.arange(blocks_dev)[:, None]).astype(
        jnp.float32
    )
    gathered = jnp.dot(
        owner_hot, back_sums.reshape(devices * CAP, BLK * D), precision=lax.Precision.HIGHEST
    )
    gathered_mass = jnp.dot(
        owner_hot, back_mass.reshape(devices * CAP, BLK), precision=lax.Precision.HIGHEST
    )
    level1_new = (centroids1.astype(jnp.float32) + gathered.reshape(K1_DEV, D)) / (
        1.0 + gathered_mass.reshape(K1_DEV, 1)
    )
    shard_rows = K2 // sub_count

    def partial_block(shard_index):
        hot_two = weighted_hot(level2_ids - shard_index * shard_rows, shard_rows, weights_low)
        return (column_sums(hot_two, points), jnp.sum(hot_two.astype(jnp.float32), axis=0))

    block_sums, block_mass = lax.map(partial_block, jnp.arange(sub_count))
    sums_two, mass_two = (
        lax.psum_scatter(
            block_sums.reshape(K2, D).astype(jnp.bfloat16), "sub", scatter_dimension=0, tiled=True
        ).astype(jnp.float32),
        lax.psum_scatter(
            block_mass.reshape(K2).astype(jnp.bfloat16), "sub", scatter_dimension=0, tiled=True
        ).astype(jnp.float32),
    )
    level2_new = ((centroids2[0].astype(jnp.float32) + sums_two) / (1.0 + mass_two[:, None]))[None]
    hot_three = weighted_hot(level3_ids, K3, weights_low)
    sums_three, mass_three = lax.psum(
        (column_sums(hot_three, points), jnp.sum(hot_three.astype(jnp.float32), axis=0)),
        ("grp", "sub"),
    )
    level3_new = (centroids3.astype(jnp.float32) + sums_three) / (1.0 + mass_three[:, None])
    return (level1_new, level2_new, level3_new)


def solution(mesh):
    placed = (
        P(("grp", "sub"), None),
        P(("grp", "sub")),
        P(("grp", "sub")),
        P(("grp", "sub")),
        P(("grp", "sub"), None),
        P(("grp", "sub"), None),
        P("grp", "sub", None),
        P(),
    )
    return jax.shard_map(
        shards,
        mesh=mesh,
        in_specs=placed,
        out_specs=(P(("grp", "sub"), None), P("grp", "sub", None), P()),
        check_vma=False,
    )
```

profile of v0, /device:TPU:0, one launch (start us, length us, event | category | flops | bytes accessed | tf_op | source)
XLA Modules:
  0.0 526.9 jit_solution(3734829339410041527)
XLA Ops:
  11.5 11.2 %all-to-all-start = ((s32[128,1,2]{2,1,0:T(1,128)}), s32[128,1,2]{2,1,0:T(1,128)S(1)}, u32[]{:S(2)}, u32[]{:S(2)}) async-start(s32[128,1,2]{2,1,0:T(1,128)} %bitcast.7), calls=%async_computation | async-start | bytes 131072 | tf_op jit(solution)/shard_map/all_to_all | solution.py:39
  22.7 7.4 %reshape.227 = bf16[256,8192]{1,0:T(8,128)(2,1)} reshape(bf16[2048,1024]{1,0:T(8,128)(2,1)} %param.15) | data formatting | bytes 8388608 | tf_op jit(solution)/shard_map/reshape | solution.py:38
  32.3 11.6 %gather_fusion = bf16[256,8192]{1,0:T(8,128)(2,1)} fusion(bf16[256,8192]{1,0:T(8,128)(2,1)} %reshape.227, s32[1024]{0:T(1024)S(1)} %pad_clamp_fusion), kind=kCustom, calls=%fused_computation | custom fusion | bytes 8389632 | tf_op jit(solution)/shard_map/gather | solution.py:43
  44.0 7.6 %reshape.235 = bf16[128,2,8192]{2,1,0:T(2,128)(2,1)} reshape(bf16[256,8192]{1,0:T(8,128)(2,1)} %gather_fusion) | data formatting | bytes 8388608 | tf_op jit(solution)/shard_map/gather | solution.py:43
  51.6 8.2 %all-to-all-start.1 = ((bf16[128,2,8192]{2,1,0:T(2,128)(2,1)}), bf16[128,2,8192]{2,1,0:T(2,128)(2,1)}, u32[]{:S(2)}, u32[]{:S(2)}) async-start(bf16[128,2,8192]{2,1,0:T(2,128)(2,1)} %reshape.235), calls=%async_computation.1 | async-start | bytes 8388608 | tf_op jit(solution)/shard_map/all_to_all | solution.py:42
  60.5 50.7 %all-to-all-done.1 = bf16[128,2,8192]{2,1,0:T(2,128)(2,1)} async-done(((bf16[128,2,8192]{2,1,0:T(2,128)(2,1)}), bf16[128,2,8192]{2,1,0:T(2,128)(2,1)}, u32[]{:S(2)}, u32[]{:S(2)}) %all-to-all-start.1) | async-done | bytes 4194336 | tf_op jit(solution)/shard_map/all_to_all | solution.py:42
  111.2 7.8 %reshape.228 = bf16[2048,1024]{1,0:T(8,128)(2,1)} reshape(bf16[128,2,8192]{2,1,0:T(2,128)(2,1)} %all-to-all-done.1) | data formatting | bytes 8388608 | tf_op jit(solution)/shard_map/reshape | solution.py:45
  119.0 7.7 %gather_fusion.1 = bf16[1024,1024]{1,0:T(8,128)(2,1)S(1)} fusion(bf16[2048,1024]{1,0:T(8,128)(2,1)} %reshape.228, s32[1024]{0:T(1024)S(1)} %get-tuple-element.57), kind=kCustom, calls=%fused_computation.1 | custom fusion | bytes 4198400 | tf_op jit(solution)/shard_map/gather | solution.py:49
  126.7 2.5 multiply_reduce_fusion
  131.4 65.2 %while.12 = (s32[]{:T(128)}, bf16[16,512,1024]{2,1,0:T(8,128)(2,1)}, bf16[16,512]{1,0:T(8,128)(2,1)S(1)}, s32[16]{0:T(128)S(1)}, s32[1024]{0:T(1024)S(1)}, /*ind...) while((s32[]{:T(128)}, ...), condition=%wide.region_8.9_spmd, body=%wide.region_6.8_spmd.sunk | while | flops 1076888064 | bytes 4221573 | solution.py:90
  132.6 2.4 bitcast_dynamic-update-slice_fusion.2
  136.7 2.4 bitcast_dynamic-update-slice_fusion.2
  140.8 2.4 bitcast_dynamic-update-slice_fusion.2
  144.9 2.4 bitcast_dynamic-update-slice_fusion.2
  153.0 2.4 bitcast_dynamic-update-slice_fusion.2
  157.1 2.4 bitcast_dynamic-update-slice_fusion.2
  165.2 2.5 bitcast_dynamic-update-slice_fusion.2
  169.4 2.4 bitcast_dynamic-update-slice_fusion.2
  173.4 2.4 bitcast_dynamic-update-slice_fusion.2
  181.6 2.5 bitcast_dynamic-update-slice_fusion.2
  189.7 2.4 bitcast_dynamic-update-slice_fusion.2
  193.8 2.4 bitcast_dynamic-update-slice_fusion.2
  198.6 5.0 all-to-all-start.3
  203.6 7.1 %fusion.7 = f32[2048,1024]{1,0:T(8,128)} fusion(bf16[1024,1024]{1,0:T(8,128)(2,1)S(1)} %get-tuple-element.140, s32[1024]{0:T(1024)S(1)} %get-tuple-element.58, bf16[1024]{0:T(1024)(128)(2,1)S(1)} %get-tuple-element.149), kind=kOutput, calls=%fused_computation.16 | convolution fusion | flops 4299161600 | bytes 10491904 | tf_op jit(solution)/shard_map/dot_general | solution.py:23
  213.1 7.9 %all-to-all-start.2 = ((f32[128,16,1024]{2,1,0:T(8,128)}), f32[128,16,1024]{2,1,0:T(8,128)}, u32[]{:S(2)}, u32[]{:S(2)}) async-start(f32[128,16,1024]{2,1,0:T(8,128)} %bitcast.72), calls=%async_computation.2 | async-start | bytes 16777216 | tf_op jit(solution)/shard_map/all_to_all | solution.py:57
  224.1 177.3 %psum.15 = f32[256]{0:T(256)S(1)} all-reduce(f32[256]{0:T(256)S(1)} %convert_reduce_fusion.2), channel_id=1, replica_groups=mesh['grp'=8,'sub'=16] {'grp','sub'}, use_global_device_ids=true, to_apply=%region_13.14 | all-reduce | flops 256 | bytes 2048 | tf_op jit(solution)/shard_map/psum | solution.py:101
  401.4 72.1 %all-reduce = bf16[8192]{0:T(1024)(128)(2,1)S(1)} all-reduce(bf16[8192]{0:T(1024)(128)(2,1)S(1)} %bitcast.75), channel_id=3, replica_groups=mesh['grp'=8,'sub'=16] {'sub'}, use_global_device_ids=true, to_apply=%region_10.11.clone | all-reduce | flops 8192 | bytes 32768
  477.9 9.4 %reshape.230 = f32[256,8192]{1,0:T(8,128)} reshape(f32[128,16,1024]{2,1,0:T(8,128)} %all-to-all-done.2) | data formatting | bytes 16777216 | tf_op jit(solution)/shard_map/reshape | solution.py:76
  487.3 12.0 %fusion.20 = f32[256,8192]{1,0:T(8,128)} fusion(f32[256,8192]{1,0:T(8,128)} %reshape.230, s32[256]{0:T(256)S(1)} %eq.52), kind=kOutput, calls=%fused_computation.36 | convolution fusion | flops 6442516480 | bytes 16778240 | tf_op jit(solution)/shard_map/dot_general | solution.py:75
  499.3 9.4 %reshape.231 = f32[2048,1024]{1,0:T(8,128)} reshape(f32[256,8192]{1,0:T(8,128)} %fusion.20) | data formatting | bytes 16777216 | tf_op jit(solution)/shard_map/reshape | solution.py:81
  508.7 7.8 %add_divide_fusion = f32[2048,1024]{1,0:T(8,128)} fusion(f32[2048,1024]{1,0:T(8,128)} %reshape.231, bf16[2048,1024]{1,0:T(8,128)(2,1)} %param.15, f32[2048]{0:T(1024)S(1)} %add.158), kind=kLoop, calls=%fused_computation.13 | loop fusion | flops 6291456 | bytes 20979712 | tf_op jit(solution)/shard_map/div | solution.py:81
  516.4 3.0 fusion.11
  (131 shorter events, 44.8 us)
Async XLA Ops:
  11.5 20.6 %all-to-all-start = ((s32[128,1,2]{2,1,0:T(1,128)}), s32[128,1,2]{2,1,0:T(1,128)S(1)}, u32[]{:S(2)}, u32[]{:S(2)}) async-start(s32[128,1,2]{2,1,0:T(1,128)} %bitcast.7), calls=%async_computation | async-start | bytes 131072 | tf_op jit(solution)/shard_map/all_to_all | solution.py:39
  51.6 8.5 %copy-start.7 = (s32[1,128]{1,0:T(1,128)S(1)}, s32[1,128]{1,0:T(1,128)}, u32[]{:S(2)}) copy-start(s32[1,128]{1,0:T(1,128)} %param.14) | copy-start | bytes 1540
  51.6 8.5 %copy-start.6 = (s32[1024]{0:T(1024)S(1)}, s32[1024]{0:T(1024)}, u32[]{:S(2)}) copy-start(s32[1024]{0:T(1024)} %param.11) | copy-start | bytes 12292
  51.6 59.7 %all-to-all-start.1 = ((bf16[128,2,8192]{2,1,0:T(2,128)(2,1)}), bf16[128,2,8192]{2,1,0:T(2,128)(2,1)}, u32[]{:S(2)}, u32[]{:S(2)}) async-start(bf16[128,2,8192]{2,1,0:T(2,128)(2,1)} %reshape.235), calls=%async_computation.1 | async-start | bytes 8388608 | tf_op jit(solution)/shard_map/all_to_all | solution.py:42
  59.8 415.7 %all-reduce.3.cloned.1.call-start = ((), (), s32[]{:S(2)}) async-start(), calls=%async_computation.6 | async-start | bytes 2097152 | tf_op jit(solution)/shard_map/psum | solution.py:101
  126.7 2.5 copy-start
  126.7 2.5 copy-start.5
  126.7 4.6 copy-start.4
  129.2 2.1 copy-start.1
  131.3 385.1 %reduce-scatter.2.cloned.1.call-start = ((), (), s32[]{:S(2)}) async-start(), calls=%async_computation.5 | async-start | bytes 17825792 | tf_op jit(solution)/shard_map/reduce_scatter | solution.py:92
  198.6 14.5 %all-to-all-start.3 = ((f32[128,1,16]{2,1,0:T(1,128)}), f32[128,1,16]{2,1,0:T(1,128)S(1)}, u32[]{:S(2)}, u32[]{:S(2)}) async-start(f32[128,1,16]{2,1,0:T(1,128)} %bitcast.12), calls=%async_computation.3 | async-start | bytes 131072 | tf_op jit(solution)/shard_map/all_to_all | solution.py:64
  213.1 8.0 %copy-start.8 = (u32[128]{0:T(128)S(1)}, u32[128]{0:T(128)}, u32[]{:S(2)}) copy-start(u32[128]{0:T(128)} %constant.105) | copy-start | bytes 1540
  213.1 262.4 %copy-start.3 = (bf16[256,1024]{1,0:T(8,128)(2,1)S(1)}, bf16[256,1024]{1,0:T(8,128)(2,1)}, u32[]{:S(2)}) copy-start(bf16[256,1024]{1,0:T(8,128)(2,1)} %param.17) | copy-start | bytes 1572868
  213.1 264.8 %all-to-all-start.2 = ((f32[128,16,1024]{2,1,0:T(8,128)}), f32[128,16,1024]{2,1,0:T(8,128)}, u32[]{:S(2)}, u32[]{:S(2)}) async-start(f32[128,16,1024]{2,1,0:T(8,128)} %bitcast.72), calls=%async_computation.2 | async-start | bytes 16777216 | tf_op jit(solution)/shard_map/all_to_all | solution.py:57
  508.7 7.8 %copy-start.2 = (bf16[1,512,1024]{2,1,0:T(8,128)(2,1)S(1)}, bf16[1,512,1024]{2,1,0:T(8,128)(2,1)}, u32[]{:S(2)}) copy-start(bf16[1,512,1024]{2,1,0:T(8,128)(2,1)} %param.16) | copy-start | bytes 3145732
Sparse Core Ops, SparseCore 0:
  131.4 248.6 all-reduce.2
Sparse Core Ops, SparseCore 1:
  196.7 209.1 reduce-scatter.1
where the time goes:
time: 529 us; the launch traced here: 527 us
  blocking collectives  249 us (47%)
  local copies, waits for them, and re-layouts  75.6 us (14%)
  matrix products  60 us (11%)
  waiting for transfers between devices  55.2 us (10%)
  starting transfers between devices  32.6 us (6%)
  other arithmetic  26.7 us (5%)
  between operations  16.4 us (3%)
  loops' own time  10.9 us (2%)
    psum x1, blocking collectives, shards(): lax.psum((column_sums(hot_three, points), jnp.sum(hot_three.astype(jnp.fl...  177 us
    unnamed x1, blocking collectives  72.1 us
    all_to_all x1, waiting for transfers between devices, shards(): lax.all_to_all(block_table[flat_asked], ('grp', 'sub'), split_axis=0, con...  50.7 us
    dot_general x18, matrix products, column_sums(): lax.dot_general(hot_table, points, (((0,), (0,)), ((), ())), preferred_el...  47.7 us
    gather x2, local copies, waits for them, and re-layouts, shards(): block_table[flat_asked]  19.3 us
    dot_general x1, matrix products, shards(): jnp.dot(owner_hot, back_sums.reshape(devices * CAP, BLK * D), precision=l...  12 us
    all_to_all x1, starting transfers between devices, shards(): lax.all_to_all(requests.reshape(devices, 1, CAP), ('grp', 'sub'), split_a...  11.2 us
    another operation x1, loops' own time, shards(): block_sums, block_mass = lax.map(partial_block, jnp.arange(sub_count))  10.9 us
  transfers between devices with their start and end apart: 6, of which 3 were waited for; matrix products, arithmetic and copies ran while one was open for 22% of the time, Pallas kernels for 0%

commit v1 on v0

v1 whole, which is shorter than its diff:
```python
import jax
import jax.numpy as jnp
from jax import lax
from jax.experimental import pallas as pl
from jax.experimental.pallas import tpu as pltpu
from jax.sharding import PartitionSpec as P

D = 1024
K1_DEV = 2048
BLK = 8
CAP = 2
K2 = 8192
K3 = 256
CAP2 = 128
TILE = 256
BF = jnp.bfloat16
F32 = jnp.float32
I32 = jnp.int32


def full(shape):
    return pl.BlockSpec(shape, lambda *_: (0,) * len(shape))


ANY = pl.BlockSpec(memory_space=pl.ANY)


def iota(shape, axis):
    return lax.broadcasted_iota(I32, shape, axis)


def route_kernel(ids_ref, pts_ref, out_ref, rank_ref, local_ref, slot_scr):
    step = pl.program_id(0)
    n = pts_ref.shape[0]
    subs = local_ref.shape[0]
    rows = K2 // subs
    chunk = out_ref.shape[0]

    @pl.when(step == 0)
    def _():
        ids = ids_ref[...]
        owner = ids // rows
        local = ids - owner * rows
        hot = (jnp.broadcast_to(owner, (subs, n)) == iota((subs, n), 0)).astype(F32)
        upper = (iota((n, n), 0) < iota((n, n), 1)).astype(F32).astype(BF)
        before = jnp.dot(hot.astype(BF), upper, preferred_element_type=F32)
        rank = jnp.sum(before * hot, axis=0, keepdims=True)
        slot_scr[...] = owner * CAP2 + rank.astype(I32)
        rank_col = jnp.transpose(jnp.broadcast_to(rank, (128, n)))
        rank_ref[...] = rank_col.astype(I32)
        hot_rank = (rank_col.astype(I32) == iota((n, CAP2), 1)).astype(F32).astype(BF)
        high = local // 256
        low = local - high * 256
        low_hot = (hot * low.astype(F32)).astype(BF)
        high_hot = (hot * high.astype(F32)).astype(BF)
        local_ref[...] = jnp.dot(low_hot, hot_rank, preferred_element_type=F32) + 256.0 * jnp.dot(
            high_hot, hot_rank, preferred_element_type=F32
        )

    slots = jnp.broadcast_to(slot_scr[...], (chunk, n))
    perm = (slots == iota((chunk, n), 0) + step * chunk).astype(F32).astype(BF)
    out_ref[...] = jnp.dot(perm, pts_ref[...], preferred_element_type=F32).astype(BF)


def route(ids2, points, subs):
    n = points.shape[0]
    total = subs * CAP2
    chunk = 512
    return pl.pallas_call(
        route_kernel,
        grid=(total // chunk,),
        in_specs=[full((1, n)), full((n, D))],
        out_specs=[
            pl.BlockSpec((chunk, D), lambda i: (i, 0)),
            full((n, 128)),
            full((subs, CAP2)),
        ],
        out_shape=[
            jax.ShapeDtypeStruct((total, D), BF),
            jax.ShapeDtypeStruct((n, 128), I32),
            jax.ShapeDtypeStruct((subs, CAP2), F32),
        ],
        scratch_shapes=[pltpu.VMEM((1, n), I32)],
        name="route",
    )(ids2.reshape(1, n), points)


def serve_kernel(asked, table_ref, out_ref, sem):
    count = out_ref.shape[0]

    def one(i, carry):
        pltpu.make_async_copy(table_ref.at[jnp.maximum(asked[i], 0)], out_ref.at[i], sem).start()
        return carry

    lax.fori_loop(0, count, one, 0, unroll=8)
    pltpu.make_async_copy(out_ref, out_ref, sem).wait()


def serve(asked, table):
    return pl.pallas_call(
        serve_kernel,
        grid_spec=pltpu.PrefetchScalarGridSpec(
            num_scalar_prefetch=1,
            grid=(),
            in_specs=[pl.BlockSpec(memory_space=pltpu.VMEM)],
            out_specs=ANY,
            scratch_shapes=[pltpu.SemaphoreType.DMA],
        ),
        out_shape=jax.ShapeDtypeStruct((asked.shape[0], BLK, D), BF),
        name="serve",
    )(asked, table)


def weigh_kernel(
    slot, fetched_ref, col1_ref, row1_ref, row2_ref, row3_ref, rank_ref, local_ref, pts_ref,
    sums_ref, small_ref, meta_ref,
    near_scr, sum_scr, w_scr, ext_scr, sem_in, sem_out,
):
    n = pts_ref.shape[0]
    need = near_scr.shape[0]
    rows = need * BLK

    def fetch(e, carry):
        pltpu.make_async_copy(fetched_ref.at[slot[e]], near_scr.at[e], sem_in).start()
        return carry

    lax.fori_loop(0, need, fetch, 0, unroll=8)
    ext_scr[...] = jnp.zeros(ext_scr.shape, F32)
    pltpu.make_async_copy(near_scr, near_scr, sem_in).wait()
    near = near_scr[...].reshape(rows, D)
    step = 256
    for c in range(n // step):
        col = col1_ref[c * step : (c + 1) * step, :]
        hot = jnp.concatenate(
            [(col == iota((step, 128), 1) + 128 * t).astype(F32) for t in range(rows // 128)], axis=1
        ).astype(BF)
        nearest = jnp.dot(hot, near, preferred_element_type=F32)
        diff = pts_ref[c * step : (c + 1) * step, :].astype(F32) - nearest
        spread = jnp.sum(diff * diff, axis=1, keepdims=True) / D
        w = (1.0 / (1.0 + spread)).astype(BF).astype(F32)
        w_scr[c * step : (c + 1) * step, :] = jnp.broadcast_to(w, (step, 128))
    w_col = w_scr[...]
    w_row = jnp.transpose(w_col)[0:1, :]

    def weighted(row_ids, count, first):
        same = jnp.broadcast_to(row_ids, (count, n)) == iota((count, n), 0) + first
        return jnp.where(same, jnp.broadcast_to(w_row, (count, n)), 0.0)

    lane = iota((BLK, 128), 1)
    tile = iota((K3, 128), 1)

    hot3 = weighted(row3_ref[...], K3, 0)
    sums3 = jnp.dot(hot3.astype(BF), pts_ref[...], preferred_element_type=F32).astype(BF)
    mass3 = jnp.broadcast_to(jnp.sum(hot3, axis=1, keepdims=True), (K3, 128))
    high3 = mass3.astype(BF).astype(F32)
    ext3 = jnp.where(tile == 4, high3, 0.0) + jnp.where(tile == 5, mass3 - high3, 0.0)
    wide = D // TILE
    devices = small_ref.shape[0]
    for o in range(devices):
        b, c = o // wide, o % wide
        small_ref[o, :, 0:TILE] = sums3[BLK * b : BLK * (b + 1), TILE * c : TILE * (c + 1)]

    part = 256
    for c in range(rows // part):
        hot1 = weighted(row1_ref[...], part, c * part)
        sums1 = jnp.dot(hot1.astype(BF), pts_ref[...], preferred_element_type=F32).astype(BF)
        sum_scr[c * (part // BLK) : (c + 1) * (part // BLK)] = sums1.reshape(part // BLK, BLK, D)
        mass1 = jnp.broadcast_to(jnp.sum(hot1, axis=1, keepdims=True), (part, 128))
        for k in range(part // BLK):
            e = c * (part // BLK) + k
            s = slot[e]
            pltpu.make_async_copy(sum_scr.at[e], sums_ref.at[s], sem_out).start()
            m = mass1[k * BLK : (k + 1) * BLK, :]
            high = m.astype(BF).astype(F32)
            o = s // CAP
            at = (s - o * CAP) * 2
            ext_scr[o] = ext_scr[o] + jnp.where(lane == at, high, 0.0) + jnp.where(
                lane == at + 1, m - high, 0.0
            )
    for o in range(devices):
        b = o // wide
        small_ref[o, :, TILE:] = (ext_scr[o] + ext3[BLK * b : BLK * (b + 1), :]).astype(BF)

    subs = meta_ref.shape[0]
    owner = row2_ref[...] // (K2 // subs)
    hot_owner = (jnp.broadcast_to(owner, (subs, n)) == iota((subs, n), 0)).astype(F32).astype(BF)
    hot_rank = jnp.where(rank_ref[...] == iota((n, CAP2), 1), w_col, 0.0).astype(BF)
    w_slots = jnp.dot(hot_owner, hot_rank, preferred_element_type=F32)
    meta_ref[...] = jnp.zeros(meta_ref.shape, F32)
    for t in range(subs):
        meta_ref[t, 0:1, :] = w_slots[t : t + 1, :]
        meta_ref[t, 1:2, :] = local_ref[t : t + 1, :]
    pltpu.make_async_copy(sum_scr, sum_scr, sem_out).wait()


def weigh(slot, fetched, ids1, ids2, ids3, rank, local, points, devices):
    n = points.shape[0]
    need = slot.shape[0]
    subs = local.shape[0]
    return pl.pallas_call(
        weigh_kernel,
        grid_spec=pltpu.PrefetchScalarGridSpec(
            num_scalar_prefetch=1,
            grid=(1,),
            in_specs=[
                ANY,
                full((n, 128)),
                full((1, n)),
                full((1, n)),
                full((1, n)),
                full((n, 128)),
                full((subs, CAP2)),
                full((n, D)),
            ],
            out_specs=[
                ANY,
                full((devices, BLK, TILE + 128)),
                full((subs, BLK, CAP2)),
            ],
            scratch_shapes=[
                pltpu.VMEM((need, BLK, D), BF),
                pltpu.VMEM((need, BLK, D), BF),
                pltpu.VMEM((n, 128), F32),
                pltpu.VMEM((devices, BLK, 128), F32),
                pltpu.SemaphoreType.DMA,
                pltpu.SemaphoreType.DMA,
            ],
        ),
        out_shape=[
            jax.ShapeDtypeStruct(fetched.shape, BF),
            jax.ShapeDtypeStruct((devices, BLK, TILE + 128), BF),
            jax.ShapeDtypeStruct((subs, BLK, CAP2), F32),
        ],
        name="weigh",
    )(
        slot,
        fetched,
        jnp.broadcast_to(ids1[:, None], (n, 128)),
        ids1.reshape(1, n),
        ids2.reshape(1, n),
        ids3.reshape(1, n),
        rank,
        local,
        points,
    )


def level3_kernel(place, small_ref, cent_ref, out_ref):
    total = jnp.sum(small_ref[...].astype(F32), axis=0)
    lane = iota((BLK, 128), 1)
    ext = total[:, TILE:]
    mass = jnp.sum(jnp.where((lane == 4) | (lane == 5), ext, 0.0), axis=1, keepdims=True)
    new = (cent_ref[...].astype(F32) + total[:, 0:TILE]) / (1.0 + mass)
    out_ref[...] = jnp.broadcast_to(new.astype(BF)[None], out_ref.shape)


def level3(me, small, centroids3):
    devices = small.shape[0]
    wide = D // TILE
    return pl.pallas_call(
        level3_kernel,
        grid_spec=pltpu.PrefetchScalarGridSpec(
            num_scalar_prefetch=1,
            grid=(1,),
            in_specs=[
                full(small.shape),
                pl.BlockSpec((BLK, TILE), lambda i, place: (place[0], place[1])),
            ],
            out_specs=full((devices, BLK, TILE)),
        ),
        out_shape=jax.ShapeDtypeStruct((devices, BLK, TILE), BF),
        name="level3",
    )(jnp.stack([me // wide, me % wide]).astype(I32), small, centroids3)


def level2_kernel(meta_ref, pts_ref, cent_ref, out_ref):
    step = pl.program_id(0)
    count = out_ref.shape[0]
    subs = meta_ref.shape[0]
    rows = (iota((count, CAP2), 0) + step * count).astype(F32)
    hot = jnp.concatenate(
        [
            jnp.where(
                jnp.broadcast_to(meta_ref[t, 1:2, :], (count, CAP2)) == rows,
                jnp.broadcast_to(meta_ref[t, 0:1, :], (count, CAP2)),
                0.0,
            )
            for t in range(subs)
        ],
        axis=1,
    )
    sums = jnp.dot(hot.astype(BF), pts_ref[...], preferred_element_type=F32)
    mass = jnp.sum(hot, axis=1, keepdims=True)
    out_ref[...] = (cent_ref[...].astype(F32) + sums) / (1.0 + mass)


def level2(meta, routed, centroids2):
    rows = centroids2.shape[0]
    count = 128
    return pl.pallas_call(
        level2_kernel,
        grid=(rows // count,),
        in_specs=[
            full(meta.shape),
            full(routed.shape),
            pl.BlockSpec((count, D), lambda i: (i, 0)),
        ],
        out_specs=pl.BlockSpec((count, D), lambda i: (i, 0)),
        out_shape=jax.ShapeDtypeStruct((rows, D), F32),
        name="level2",
    )(meta, routed, centroids2)


def level1_kernel(asked, back_ref, small_ref, cent_ref, out_ref, acc_scr, mass_scr, stage, sem):
    blocks = acc_scr.shape[0]
    slots = back_ref.shape[0]
    lane = iota((BLK, 128), 1)
    part = stage.shape[1]

    def begin(g, carry):
        at = pl.ds(pl.multiple_of(g * 8, 8), 8)
        acc_scr[at] = cent_ref[at].astype(F32)
        mass_scr[at] = jnp.zeros((8, BLK, 128), F32)
        return carry

    lax.fori_loop(0, blocks // 8, begin, 0)

    def add(s, carry):
        b = asked[s]

        @pl.when(b >= 0)
        def _():
            acc_scr[b] = acc_scr[b] + back_ref[s].astype(F32)
            at = (s % CAP) * 2
            m = small_ref[s // CAP, :, TILE:].astype(F32)
            mass_scr[b] = mass_scr[b] + jnp.where((lane == at) | (lane == at + 1), m, 0.0)

        return carry

    lax.fori_loop(0, slots, add, 0, unroll=4)

    for g in range(blocks // part):
        k = g % 2
        view = out_ref.at[pl.ds(g * part, part)]
        if g >= 2:
            pltpu.make_async_copy(stage.at[k], view, sem.at[k]).wait()
        total = jnp.sum(mass_scr[g * part : (g + 1) * part], axis=2, keepdims=True)
        stage[k] = acc_scr[g * part : (g + 1) * part] / (1.0 + total)
        pltpu.make_async_copy(stage.at[k], view, sem.at[k]).start()
    for k in range(2):
        pltpu.make_async_copy(stage.at[k], out_ref.at[pl.ds(0, part)], sem.at[k]).wait()


def level1(asked, back, small, table):
    blocks = table.shape[0]
    whole = pl.BlockSpec(memory_space=pltpu.VMEM)
    return pl.pallas_call(
        level1_kernel,
        grid_spec=pltpu.PrefetchScalarGridSpec(
            num_scalar_prefetch=1,
            grid=(),
            in_specs=[whole, whole, whole],
            out_specs=ANY,
            scratch_shapes=[
                pltpu.VMEM((blocks, BLK, D), F32),
                pltpu.VMEM((blocks, BLK, 128), F32),
                pltpu.VMEM((2, 32, BLK, D), F32),
                pltpu.SemaphoreType.DMA((2,)),
            ],
        ),
        out_shape=jax.ShapeDtypeStruct((blocks, BLK, D), F32),
        name="level1",
    )(asked, back, small, table)


def shards(points, level1_ids, level2_ids, level3_ids, needed, centroids1, centroids2, centroids3):
    both = ("grp", "sub")
    devices = lax.axis_size(both)
    subs = lax.axis_size("sub")
    me = lax.axis_index(both)
    blocks = K1_DEV // BLK
    wanted = needed[0]
    need = wanted.shape[0]

    def swap(values, axes):
        return lax.all_to_all(values, axes, split_axis=0, concat_axis=0, tiled=True)

    owners = wanted // blocks
    same = (owners[:, None] == owners[None, :]) & (
        jnp.arange(need)[None, :] < jnp.arange(need)[:, None]
    )
    slot = owners * CAP + jnp.sum(same.astype(I32), axis=1)
    requests = (
        jnp.sum(
            jnp.where(
                slot[:, None] == jnp.arange(devices * CAP)[None, :],
                wanted[:, None] % blocks + 1,
                0,
            ),
            axis=0,
        )
        - 1
    )
    asked = swap(requests.reshape(devices, 1, CAP), both).reshape(devices * CAP)
    routed, rank, local = route(level2_ids, points, subs)
    routed = swap(routed.reshape(subs, CAP2, D), "sub").reshape(subs * CAP2, D)
    table = centroids1.reshape(blocks, BLK, D)
    fetched = swap(serve(asked, table), both)
    sums, small, meta = weigh(
        slot, fetched, level1_ids, level2_ids, level3_ids, rank, local, points, devices
    )
    small = swap(small, both)
    back = swap(sums, both)
    meta = swap(meta, "sub")
    tiles = swap(level3(me, small, centroids3), both)
    level2_new = level2(meta, routed, centroids2[0])[None]
    level1_new = level1(asked, back, small, table).reshape(K1_DEV, D)
    wide = D // TILE
    level3_new = (
        tiles.reshape(K3 // BLK, wide, BLK, TILE).transpose(0, 2, 1, 3).reshape(K3, D).astype(F32)
    )
    return level1_new, level2_new, level3_new


def solution(mesh):
    placed = (
        P(("grp", "sub"), None),
        P(("grp", "sub")),
        P(("grp", "sub")),
        P(("grp", "sub")),
        P(("grp", "sub"), None),
        P(("grp", "sub"), None),
        P("grp", "sub", None),
        P(),
    )
    return jax.shard_map(
        shards,
        mesh=mesh,
        in_specs=placed,
        out_specs=(P(("grp", "sub"), None), P("grp", "sub", None), P()),
        check_vma=False,
    )
```

time: 529 us -> 280 us (0.53)
  blocking collectives: 249 us -> 38.9 us
  waiting for transfers between devices: 55.2 us -> 156 us
  local copies, waits for them, and re-layouts: 75.6 us -> 2.38 us
  matrix products: 60 us -> 0 us
  Pallas kernels: 0 us -> 47.9 us
  other arithmetic: 26.7 us -> 4.11 us
  between operations: 16.4 us -> 0.77 us
  loops' own time: 10.9 us -> 0 us
    psum x1 -> x0, blocking collectives: 177 us -> none  [shards(): lax.psum((column_sums(hot_three, points), jnp.sum(hot_three.astype(jnp.fl...]
    all_to_all x4 -> x5, waiting for transfers between devices: 55.2 us -> 156 us  [swap(): return lax.all_to_all(values, axes, split_axis=0, concat_axis=0, tiled=True)]
    unnamed x1 -> x0, blocking collectives: 72.1 us -> none
    dot_general x20 -> x0, matrix products: 60 us -> none  [the longest x18 47.7 us: column_sums(): lax.dot_general(hot_table, points, (((0,), (0,)), ((), ())), preferred_el...]
    pallas_call x0 -> x6, Pallas kernels: none -> 47.9 us  [the longest x1 13.4 us: level1(): pl.pallas_call(level1_kernel, grid_spec=pltpu.PrefetchScalarGridSpec(num_...]
    all_to_all x0 -> x2, blocking collectives: none -> 38.9 us  [swap(): return lax.all_to_all(values, axes, split_axis=0, concat_axis=0, tiled=True)]
    reshape x6 -> x1, local copies, waits for them, and re-layouts: 34.7 us -> 0.72 us  [shards(): asked = swap(requests.reshape(devices, 1, CAP), both).reshape(devices * CAP)]
    gather x3 -> x0, local copies, waits for them, and re-layouts: 27 us -> none  [the longest x2 19.3 us: shards(): block_table[flat_asked]]
  transfers between devices with their start and end apart: 6 -> 5, of which waited for: 3 -> 5; matrix products, arithmetic and copies ran while one was open for 22% -> 1% of each run, Pallas kernels for 0% -> 11%
where the time goes in v1:
time: 280 us; the launch traced here: 279 us
  waiting for transfers between devices  156 us (56%)
  Pallas kernels  47.9 us (17%)
  blocking collectives  38.9 us (14%)
  starting transfers between devices  29 us (10%)
  other arithmetic  4.11 us (1%)
    all_to_all x5, waiting for transfers between devices, swap(): return lax.all_to_all(values, axes, split_axis=0, concat_axis=0, tiled=True)  156 us
    all_to_all x2, blocking collectives, swap(): return lax.all_to_all(values, axes, split_axis=0, concat_axis=0, tiled=True)  38.9 us
    all_to_all x5, starting transfers between devices, swap(): return lax.all_to_all(values, axes, split_axis=0, concat_axis=0, tiled=True)  29 us
    pallas_call x1, Pallas kernels, level1(): pl.pallas_call(level1_kernel, grid_spec=pltpu.PrefetchScalarGridSpec(num_...  13.4 us
    pallas_call x1, Pallas kernels, weigh(): pl.pallas_call(weigh_kernel, grid_spec=pltpu.PrefetchScalarGridSpec(num_s...  12 us
    pallas_call x1, Pallas kernels, route(): pl.pallas_call(route_kernel, grid=(total // chunk,), in_specs=[full((1, n...  8.29 us
    pallas_call x1, Pallas kernels, level2(): pl.pallas_call(level2_kernel, grid=(rows // count,), in_specs=[full(meta....  6.55 us
  transfers between devices with their start and end apart: 5, of which 5 were waited for; matrix products, arithmetic and copies ran while one was open for 1% of the time, Pallas kernels for 11%

profile of v1, /device:TPU:0, one launch (start us, length us, event | category | flops | bytes accessed | tf_op | source)
XLA Modules:
  0.0 278.9 jit_solution(2373703854235335256)
XLA Ops:
  0.6 0.7 fusion.2
  1.3 0.7 and_select_fusion.2
  2.0 0.2 convert_reduce_fusion
  2.1 0.0 copy-start.3
  2.2 0.1 select_reduce_fusion
  2.3 0.1 sub.21
  2.4 20.5 %all_to_all.35 = s32[128,1,2]{2,1,0:T(1,128)S(1)} all-to-all(s32[128,1,2]{2,1,0:T(1,128)S(1)} %bitcast.42), channel_id=1, replica_groups=mesh['grp'=8,'sub'=16] {'grp','sub'}, dimensions={0} | all-to-all | bytes 2048 | tf_op jit(solution)/shard_map/all_to_all | solution.py:386
  22.9 0.5 broadcast.139
  23.4 0.8 reduce.3
  24.2 0.7 reshape.122.asked
  25.0 4.8 %serve.1 = bf16[256,8,1024]{2,1,0:T(8,128)(2,1)} custom-call(s32[256]{0:T(256)} %reshape.122.asked, bf16[256,8,1024]{2,1,0:T(8,128)(2,1)} %bitcast.34), custom_call_target="tpu_custom_call" | custom-call | tf_op jit(solution)/shard_map/serve/pallas_call | solution.py:100
  29.8 0.0 copy-done.3
  29.8 5.9 %all-to-all-start.1 = ((bf16[256,8,1024]{2,1,0:T(8,128)(2,1)}), bf16[256,8,1024]{2,1,0:T(8,128)(2,1)}, u32[]{:S(2)}, u32[]{:S(2)}) async-start(bf16[256,8,1024]{2,1,0:T(8,128)(2,1)} %serve.1), calls=%async_computation.1 | async-start | bytes 8388608 | tf_op jit(solution)/shard_map/all_to_all | solution.py:386
  35.7 8.3 %route.1 = (bf16[2048,1024]{1,0:T(8,128)(2,1)}, s32[1024,128]{1,0:T(8,128)}, f32[16,128]{1,0:T(8,128)}) custom-call(s32[1,1024]{1,0:T(1,128)} %bitcast.44, bf16[1024,1024]{1,0:T(8,128)(2,1)} %pts_ref.3), custom_call_target="tpu_custom_call" | custom-call | tf_op jit(solution)/shard_map/route/pallas_call | solution.py:69
  44.0 43.1 %all-to-all-done.1.fetched_ref = bf16[256,8,1024]{2,1,0:T(8,128)(2,1)} async-done(((bf16[256,8,1024]{2,1,0:T(8,128)(2,1)}), bf16[256,8,1024]{2,1,0:T(8,128)(2,1)}, u32[]{:S(2)}, u32[]{:S(2)}) %all-to-all-start.1) | async-done | bytes 4194336 | tf_op jit(solution)/shard_map/all_to_all | solution.py:386
  87.1 4.7 %all-to-all-start.5 = ((bf16[16,128,1024]{2,1,0:T(8,128)(2,1)}), bf16[16,128,1024]{2,1,0:T(8,128)(2,1)}, u32[]{:S(2)}, u32[]{:S(2)}) async-start(bf16[16,128,1024]{2,1,0:T(8,128)(2,1)} %bitcast.37), calls=%async_computation.5 | async-start | bytes 8388608 | tf_op jit(solution)/shard_map/all_to_all | solution.py:386
  91.8 0.0 copy-done.2
  91.8 1.0 broadcast_in_dim.18.col1_ref
  92.8 12.0 %weigh.1 = (bf16[256,8,1024]{2,1,0:T(8,128)(2,1)}, bf16[128,8,384]{2,1,0:T(8,128)(2,1)}, f32[16,8,128]{2,1,0:T(8,128)}) custom-call(s32[128]{0:T(128)} %copy-done.3, bf16[256,8,1024]{2,1,0:T(8,128)(2,1)} %all-to-all-done.1.fetched_ref, s32[1024,128]{1,0:T(8,128)} %broadcast_in_dim.18.col1_ref, s32[1,1024]{1,0:T(1,128)} %bitcast.43, s32[1,1024]{1,0:T(1,128)} %bitcast.45, ...), custom_call_target="tpu_custom_call" | custom-call | tf_op jit(solution)/shard_map/weigh/pallas_call | solution.py:200
  104.8 48.5 %all-to-all-done.5 = bf16[16,128,1024]{2,1,0:T(8,128)(2,1)} async-done(((bf16[16,128,1024]{2,1,0:T(8,128)(2,1)}), bf16[16,128,1024]{2,1,0:T(8,128)(2,1)}, u32[]{:S(2)}, u32[]{:S(2)}) %all-to-all-start.5) | async-done | bytes 4194336 | tf_op jit(solution)/shard_map/all_to_all | solution.py:386
  153.3 9.1 %all-to-all-start.3 = ((bf16[128,8,384]{2,1,0:T(8,128)(2,1)}), bf16[128,8,384]{2,1,0:T(8,128)(2,1)S(1)}, u32[]{:S(2)}, u32[]{:S(2)}) async-start(bf16[128,8,384]{2,1,0:T(8,128)(2,1)} %get-tuple-element.12), calls=%async_computation.3 | async-start | bytes 1572864 | tf_op jit(solution)/shard_map/all_to_all | solution.py:386
  162.5 16.3 %all-to-all-done.3.small_ref = bf16[128,8,384]{2,1,0:T(8,128)(2,1)S(1)} async-done(((bf16[128,8,384]{2,1,0:T(8,128)(2,1)}), bf16[128,8,384]{2,1,0:T(8,128)(2,1)S(1)}, u32[]{:S(2)}, u32[]{:S(2)}) %all-to-all-start.3) | async-done | bytes 786464 | tf_op jit(solution)/shard_map/all_to_all | solution.py:386
  178.8 3.5 %all-to-all-start.4 = ((f32[16,8,128]{2,1,0:T(8,128)}), f32[16,8,128]{2,1,0:T(8,128)S(1)}, u32[]{:S(2)}, u32[]{:S(2)}) async-start(f32[16,8,128]{2,1,0:T(8,128)} %get-tuple-element.13), calls=%async_computation.4 | async-start | bytes 131072 | tf_op jit(solution)/shard_map/all_to_all | solution.py:386
  182.3 0.6 pad_add_fusion.place
  182.9 2.8 %level3.1 = bf16[128,8,256]{2,1,0:T(8,128)(2,1)} custom-call(s32[2]{0:T(128)} %pad_add_fusion.place, bf16[128,8,384]{2,1,0:T(8,128)(2,1)} %copy-done, bf16[256,1024]{1,0:T(8,128)(2,1)} %cent_ref.1), custom_call_target="tpu_custom_call" | custom-call | tf_op jit(solution)/shard_map/level3/pallas_call | solution.py:260
  185.7 4.2 %all-to-all-done.4.meta_ref = f32[16,8,128]{2,1,0:T(8,128)S(1)} async-done(((f32[16,8,128]{2,1,0:T(8,128)}), f32[16,8,128]{2,1,0:T(8,128)S(1)}, u32[]{:S(2)}, u32[]{:S(2)}) %all-to-all-start.4) | async-done | bytes 65568 | tf_op jit(solution)/shard_map/all_to_all | solution.py:386
  189.9 18.4 %all_to_all.36 = bf16[128,8,256]{2,1,0:T(8,128)(2,1)S(1)} all-to-all(bf16[128,8,256]{2,1,0:T(8,128)(2,1)} %level3.1), channel_id=1, replica_groups=mesh['grp'=8,'sub'=16] {'grp','sub'}, dimensions={0} | all-to-all | bytes 1048576 | tf_op jit(solution)/shard_map/all_to_all | solution.py:386
  208.3 5.8 %all-to-all-start.2 = ((bf16[256,8,1024]{2,1,0:T(8,128)(2,1)}), bf16[256,8,1024]{2,1,0:T(8,128)(2,1)}, u32[]{:S(2)}, u32[]{:S(2)}) async-start(bf16[256,8,1024]{2,1,0:T(8,128)(2,1)} %get-tuple-element.11), calls=%async_computation.2 | async-start | bytes 8388608 | tf_op jit(solution)/shard_map/all_to_all | solution.py:386
  214.1 6.5 %level2.1 = f32[512,1024]{1,0:T(8,128)} custom-call(f32[16,8,128]{2,1,0:T(8,128)} %copy-done.1, bf16[2048,1024]{1,0:T(8,128)(2,1)} %bitcast.9.pts_ref, bf16[512,1024]{1,0:T(8,128)(2,1)} %bitcast.40), custom_call_target="tpu_custom_call" | custom-call | tf_op jit(solution)/shard_map/level2/pallas_call | solution.py:300
  220.7 1.1 convert.3
  221.8 43.8 %all-to-all-done.2.back_ref = bf16[256,8,1024]{2,1,0:T(8,128)(2,1)} async-done(((bf16[256,8,1024]{2,1,0:T(8,128)(2,1)}), bf16[256,8,1024]{2,1,0:T(8,128)(2,1)}, u32[]{:S(2)}, u32[]{:S(2)}) %all-to-all-start.2) | async-done | bytes 4194336 | tf_op jit(solution)/shard_map/all_to_all | solution.py:386
  265.6 13.4 %level1.1 = f32[256,8,1024]{2,1,0:T(8,128)} custom-call(s32[256]{0:T(256)} %reshape.122.asked, bf16[256,8,1024]{2,1,0:T(8,128)(2,1)} %all-to-all-done.2.back_ref, bf16[128,8,384]{2,1,0:T(8,128)(2,1)} %copy-done, bf16[256,8,1024]{2,1,0:T(8,128)(2,1)} %bitcast.35), custom_call_target="tpu_custom_call" | custom-call | tf_op jit(solution)/shard_map/level1/pallas_call | solution.py:357
  (7 shorter events, 0.0 us)
Async XLA Ops:
  2.1 27.6 %copy-start.3 = (s32[128]{0:T(128)}, s32[128]{0:T(128)S(1)}, u32[]{:S(2)}) copy-start(s32[128]{0:T(128)S(1)} %multiply_add_fusion.slot) | copy-start | bytes 1540
  29.8 57.3 %all-to-all-start.1 = ((bf16[256,8,1024]{2,1,0:T(8,128)(2,1)}), bf16[256,8,1024]{2,1,0:T(8,128)(2,1)}, u32[]{:S(2)}, u32[]{:S(2)}) async-start(bf16[256,8,1024]{2,1,0:T(8,128)(2,1)} %serve.1), calls=%async_computation.1 | async-start | bytes 8388608 | tf_op jit(solution)/shard_map/all_to_all | solution.py:386
  87.1 4.7 %copy-start.2 = (s32[1024]{0:T(1024)S(1)}, s32[1024]{0:T(1024)}, u32[]{:S(2)}) copy-start(s32[1024]{0:T(1024)} %param.9) | copy-start | bytes 12292
  87.1 66.2 %all-to-all-start.5 = ((bf16[16,128,1024]{2,1,0:T(8,128)(2,1)}), bf16[16,128,1024]{2,1,0:T(8,128)(2,1)}, u32[]{:S(2)}, u32[]{:S(2)}) async-start(bf16[16,128,1024]{2,1,0:T(8,128)(2,1)} %bitcast.37), calls=%async_computation.5 | async-start | bytes 8388608 | tf_op jit(solution)/shard_map/all_to_all | solution.py:386
  153.3 25.4 %all-to-all-start.3 = ((bf16[128,8,384]{2,1,0:T(8,128)(2,1)}), bf16[128,8,384]{2,1,0:T(8,128)(2,1)S(1)}, u32[]{:S(2)}, u32[]{:S(2)}) async-start(bf16[128,8,384]{2,1,0:T(8,128)(2,1)} %get-tuple-element.12), calls=%async_computation.3 | async-start | bytes 1572864 | tf_op jit(solution)/shard_map/all_to_all | solution.py:386
  178.8 4.1 %copy-start = (bf16[128,8,384]{2,1,0:T(8,128)(2,1)}, bf16[128,8,384]{2,1,0:T(8,128)(2,1)S(1)}, u32[]{:S(2)}) copy-start(bf16[128,8,384]{2,1,0:T(8,128)(2,1)S(1)} %all-to-all-done.3.small_ref) | copy-start | bytes 2359300
  178.8 11.1 %all-to-all-start.4 = ((f32[16,8,128]{2,1,0:T(8,128)}), f32[16,8,128]{2,1,0:T(8,128)S(1)}, u32[]{:S(2)}, u32[]{:S(2)}) async-start(f32[16,8,128]{2,1,0:T(8,128)} %get-tuple-element.13), calls=%async_computation.4 | async-start | bytes 131072 | tf_op jit(solution)/shard_map/all_to_all | solution.py:386
  189.9 18.4 %copy-start.1 = (f32[16,8,128]{2,1,0:T(8,128)}, f32[16,8,128]{2,1,0:T(8,128)S(1)}, u32[]{:S(2)}) copy-start(f32[16,8,128]{2,1,0:T(8,128)S(1)} %all-to-all-done.4.meta_ref) | copy-start | bytes 196612
  208.3 57.3 %all-to-all-start.2 = ((bf16[256,8,1024]{2,1,0:T(8,128)(2,1)}), bf16[256,8,1024]{2,1,0:T(8,128)(2,1)}, u32[]{:S(2)}, u32[]{:S(2)}) async-start(bf16[256,8,1024]{2,1,0:T(8,128)(2,1)} %get-tuple-element.11), calls=%async_computation.2 | async-start | bytes 8388608 | tf_op jit(solution)/shard_map/all_to_all | solution.py:386

commit v2 on v1

v2 whole, which is shorter than its diff:
```python
import jax
import jax.numpy as jnp
from jax import lax
from jax.experimental import pallas as pl
from jax.experimental.pallas import tpu as pltpu
from jax.sharding import PartitionSpec as P


D = 1024
K1_DEV = 2048
BLK = 8
CAP = 2
K2 = 8192
K3 = 256
CAP2 = 128
TILE = 256
BF = jnp.bfloat16
F32 = jnp.float32
I32 = jnp.int32


def full(shape):
    return pl.BlockSpec(shape, lambda *_: (0,) * len(shape))


ANY = pl.BlockSpec(memory_space=pl.ANY)


def iota(shape, axis):
    return lax.broadcasted_iota(I32, shape, axis)


def route_kernel(place, ids_ref, pts_ref, *refs):
    pieces, (slot_ref, aux_ref, slot_scr) = refs[:-3], refs[-3:]
    n = pts_ref.shape[0]
    subs = len(pieces)
    rows = K2 // subs
    ids = ids_ref[...]
    owner = ids // rows
    local = ids - owner * rows
    hot = (jnp.broadcast_to(owner, (subs, n)) == iota((subs, n), 0)).astype(F32)
    upper = (iota((n, n), 0) < iota((n, n), 1)).astype(F32).astype(BF)
    before = jnp.dot(hot.astype(BF), upper, preferred_element_type=F32)
    rank = jnp.sum(before * hot, axis=0, keepdims=True).astype(I32)
    slot_ref[...] = owner * CAP2 + rank
    away = owner - place[0]
    away = jnp.where(away < 0, away + subs, away)
    slot_scr[...] = away * CAP2 + rank
    packed = (rank % 16) + 16 * local
    col = jnp.transpose(jnp.broadcast_to(packed.astype(F32), (128, n))).astype(I32)
    rank_col = col % 16
    local_col = col // 16
    lane = iota((n, 128), 1)
    aux = jnp.where(lane == rank_col + 8, 1, 0)
    aux = aux + jnp.where(lane == rank_col + 24, local_col % 256, 0)
    aux = aux + jnp.where(lane == rank_col + 40, local_col // 256, 0)
    aux_ref[...] = aux.astype(F32)
    group = 8
    chunk = group * CAP2
    for c in range(subs // group):
        slots = jnp.broadcast_to(slot_scr[...], (chunk, n))
        perm = (slots == iota((chunk, n), 0) + c * chunk).astype(F32).astype(BF)
        moved = jnp.dot(perm, pts_ref[...], preferred_element_type=F32).astype(BF)
        for k in range(group):
            pieces[c * group + k][...] = moved[k * CAP2 : (k + 1) * CAP2, :]


def route(place, ids2, points, subs):
    n = points.shape[0]
    out = pl.pallas_call(
        route_kernel,
        grid_spec=pltpu.PrefetchScalarGridSpec(
            num_scalar_prefetch=1,
            grid=(1,),
            in_specs=[full((1, n)), full((n, D))],
            out_specs=[full((CAP2, D))] * subs + [full((1, n)), full((n, 128))],
            scratch_shapes=[pltpu.VMEM((1, n), I32)],
        ),
        out_shape=[jax.ShapeDtypeStruct((CAP2, D), BF)] * subs
        + [jax.ShapeDtypeStruct((1, n), I32), jax.ShapeDtypeStruct((n, 128), F32)],
        name="route",
    )(place, ids2.reshape(1, n), points)
    return out[:subs], out[subs], out[subs + 1]


def serve_kernel(asked, table_ref, out_ref, sem):
    count = out_ref.shape[0]

    def one(i, carry):
        pltpu.make_async_copy(table_ref.at[jnp.maximum(asked[i], 0)], out_ref.at[i], sem).start()
        return carry

    lax.fori_loop(0, count, one, 0, unroll=8)
    pltpu.make_async_copy(out_ref, out_ref, sem).wait()


def serve(asked, table):
    return pl.pallas_call(
        serve_kernel,
        grid_spec=pltpu.PrefetchScalarGridSpec(
            num_scalar_prefetch=1,
            grid=(),
            in_specs=[pl.BlockSpec(memory_space=pltpu.VMEM)],
            out_specs=ANY,
            scratch_shapes=[pltpu.SemaphoreType.DMA],
        ),
        out_shape=jax.ShapeDtypeStruct((asked.shape[0], BLK, D), BF),
        name="serve",
    )(asked, table)


def weigh_kernel(
    slot, place, fetched_ref, col1_ref, row1_ref, row3_ref, slot2_ref, aux_ref, pts_ref, out_ref,
    near_scr, sum_scr, w_scr, ext_scr, small_scr, sem_in, sem_out,
):
    n = pts_ref.shape[0]
    need = near_scr.shape[0]
    devices = out_ref.shape[0]
    rows = need * BLK

    def fetch(e, carry):
        pltpu.make_async_copy(fetched_ref.at[slot[e]], near_scr.at[e], sem_in).start()
        return carry

    lax.fori_loop(0, need, fetch, 0, unroll=8)
    ext_scr[...] = jnp.zeros(ext_scr.shape, F32)
    pltpu.make_async_copy(near_scr, near_scr, sem_in).wait()
    near = near_scr[...].reshape(rows, D)
    step = 512
    for c in range(n // step):
        col = col1_ref[c * step : (c + 1) * step, :]
        hot = jnp.concatenate(
            [(col == iota((step, 128), 1) + 128 * t).astype(F32) for t in range(rows // 128)], axis=1
        ).astype(BF)
        nearest = jnp.dot(hot, near, preferred_element_type=F32)
        diff = pts_ref[c * step : (c + 1) * step, :].astype(F32) - nearest
        spread = jnp.sum(diff * diff, axis=1, keepdims=True) / D
        w = (1.0 / (1.0 + spread)).astype(BF).astype(F32)
        w_scr[c * step : (c + 1) * step, :] = jnp.broadcast_to(w, (step, 128))
    w_col = w_scr[...]
    w_row = jnp.transpose(w_col)[0:1, :]

    def weighted(row_ids, count, first):
        same = jnp.broadcast_to(row_ids, (count, n)) == iota((count, n), 0) + first
        return jnp.where(same, jnp.broadcast_to(w_row, (count, n)), 0.0)

    lane = iota((BLK, 128), 1)

    part = 512
    for c in range(rows // part):
        hot1 = weighted(row1_ref[...], part, c * part)
        sums1 = jnp.dot(hot1.astype(BF), pts_ref[...], preferred_element_type=F32).astype(BF)
        sum_scr[c * (part // BLK) : (c + 1) * (part // BLK)] = sums1.reshape(part // BLK, BLK, D)
        mass1 = jnp.broadcast_to(jnp.sum(hot1, axis=1, keepdims=True), (part, 128))
        for k in range(part // BLK):
            e = c * (part // BLK) + k
            s = slot[e]
            o = s // CAP
            at = s - o * CAP
            pltpu.make_async_copy(
                sum_scr.at[e], out_ref.at[o, :, pl.ds(pl.multiple_of(at * D, D), D)], sem_out
            ).start()
            m = mass1[k * BLK : (k + 1) * BLK, :]
            high = m.astype(BF).astype(F32)
            ext_scr[o] = ext_scr[o] + jnp.where(lane == 2 * at, high, 0.0) + jnp.where(
                lane == 2 * at + 1, m - high, 0.0
            )

    cells = slot2_ref[...] // 16
    count = K2 // 512 * CAP2 // 16
    hot_cell = (jnp.broadcast_to(cells, (count, n)) == iota((count, n), 0)).astype(F32).astype(BF)
    aux = aux_ref[...]
    aux = jnp.where(iota((n, 128), 1) < 24, aux * w_col, aux).astype(BF)
    table = jnp.dot(hot_cell, aux, preferred_element_type=F32)
    for t in range(count // BLK):
        o = place[1] + t
        ext_scr[o] = ext_scr[o] + table[t * BLK : (t + 1) * BLK, :]

    tile = iota((K3, 128), 1)
    hot3 = weighted(row3_ref[...], K3, 0)
    sums3 = jnp.dot(hot3.astype(BF), pts_ref[...], preferred_element_type=F32).astype(BF)
    mass3 = jnp.broadcast_to(jnp.sum(hot3, axis=1, keepdims=True), (K3, 128))
    high3 = mass3.astype(BF).astype(F32)
    ext3 = jnp.where(tile == 4, high3, 0.0) + jnp.where(tile == 5, mass3 - high3, 0.0)
    wide = D // TILE
    for o in range(devices):
        b, c = o // wide, o % wide
        small_scr[o, :, 0:TILE] = sums3[BLK * b : BLK * (b + 1), TILE * c : TILE * (c + 1)]
        small_scr[o, :, TILE:] = (ext_scr[o] + ext3[BLK * b : BLK * (b + 1), :]).astype(BF)
    tail = pltpu.make_async_copy(small_scr, out_ref.at[:, :, pl.ds(CAP * D, TILE + 128)], sem_in)
    tail.start()
    pltpu.make_async_copy(sum_scr, sum_scr, sem_out).wait()
    tail.wait()


def weigh(slot, place, fetched, ids1, ids3, slot2, aux, points, devices):
    n = points.shape[0]
    need = slot.shape[0]
    return pl.pallas_call(
        weigh_kernel,
        grid_spec=pltpu.PrefetchScalarGridSpec(
            num_scalar_prefetch=2,
            grid=(1,),
            in_specs=[
                ANY,
                full((n, 128)),
                full((1, n)),
                full((1, n)),
                full((1, n)),
                full((n, 128)),
                full((n, D)),
            ],
            out_specs=ANY,
            scratch_shapes=[
                pltpu.VMEM((need, BLK, D), BF),
                pltpu.VMEM((need, BLK, D), BF),
                pltpu.VMEM((n, 128), F32),
                pltpu.VMEM((devices, BLK, 128), F32),
                pltpu.VMEM((devices, BLK, TILE + 128), BF),
                pltpu.SemaphoreType.DMA,
                pltpu.SemaphoreType.DMA,
            ],
        ),
        out_shape=jax.ShapeDtypeStruct((devices, BLK, CAP * D + TILE + 128), BF),
        name="weigh",
    )(
        slot,
        place,
        fetched,
        jnp.broadcast_to(ids1[:, None], (n, 128)),
        ids1.reshape(1, n),
        ids3.reshape(1, n),
        slot2,
        aux,
        points,
    )


def level3_kernel(place, tile_ref, ext_ref, cent_ref, out_ref):
    total = jnp.sum(tile_ref[...].astype(F32), axis=0)
    ext = jnp.sum(ext_ref[...].astype(F32), axis=0)
    lane = iota((BLK, 128), 1)
    mass = jnp.sum(jnp.where((lane == 4) | (lane == 5), ext, 0.0), axis=1, keepdims=True)
    new = (cent_ref[...].astype(F32) + total) / (1.0 + mass)
    out_ref[...] = jnp.broadcast_to(new.astype(BF)[None], out_ref.shape)


def level3(place, back, centroids3):
    devices = back.shape[0]
    return pl.pallas_call(
        level3_kernel,
        grid_spec=pltpu.PrefetchScalarGridSpec(
            num_scalar_prefetch=1,
            grid=(1,),
            in_specs=[
                pl.BlockSpec((devices, BLK, TILE), lambda i, place: (0, 0, CAP * D // TILE)),
                pl.BlockSpec((devices, BLK, 128), lambda i, place: (0, 0, (CAP * D + TILE) // 128)),
                pl.BlockSpec((BLK, TILE), lambda i, place: (place[2], place[3])),
            ],
            out_specs=full((devices, BLK, TILE)),
        ),
        out_shape=jax.ShapeDtypeStruct((devices, BLK, TILE), BF),
        name="level3",
    )(place, back, back, centroids3)


def level2_kernel(place, ext_ref, cent_ref, *refs):
    pieces, (out_ref, pts_scr, hot_scr, w_scr, id_scr, mass_scr, sem) = refs[:-7], refs[-7:]
    rows, width = out_ref.shape
    step = pl.program_id(0)
    subs = len(pieces)

    @pl.when(step == 0)
    def _():
        for k in range(subs):
            source = place[0] - k
            source = jnp.where(source < 0, source + subs, source)
            at = pl.ds(pl.multiple_of(source * CAP2, CAP2), CAP2)
            pltpu.make_async_copy(pieces[k], pts_scr.at[at], sem).start()
        cells = ext_ref[...].astype(F32).reshape(subs * BLK, 128).astype(BF)
        lane_in = iota((128, 128), 0)
        lane_out = iota((128, 128), 1)
        own = iota((subs * BLK, 128), 1) // 16 == iota((subs * BLK, 128), 0) % BLK

        def unpack(first):
            spread = (lane_in == first + lane_out % 16).astype(F32).astype(BF)
            wide = jnp.dot(cells, spread, preferred_element_type=F32)
            return jnp.sum(jnp.where(own, wide, 0.0).reshape(subs, BLK, 128), axis=1)

        w_scr[...] = unpack(8)
        id_scr[...] = unpack(24) + 256.0 * unpack(40)
        ids = iota((rows, CAP2), 0).astype(F32)
        mass = jnp.zeros((rows, CAP2), F32)
        for t in range(subs):
            hot = jnp.where(
                jnp.broadcast_to(id_scr[t : t + 1, :], (rows, CAP2)) == ids,
                jnp.broadcast_to(w_scr[t : t + 1, :], (rows, CAP2)),
                0.0,
            )
            mass = mass + hot
            hot_scr[:, t * CAP2 : (t + 1) * CAP2] = hot.astype(BF)
        total = jnp.sum(mass, axis=1, keepdims=True)
        mass_scr[...] = jnp.broadcast_to(1.0 + total, (rows, 128))
        pltpu.make_async_copy(pts_scr, pts_scr, sem).wait()

    at = pl.ds(pl.multiple_of(step * width, width), width)
    sums = jnp.dot(hot_scr[...], pts_scr[:, at], preferred_element_type=F32)
    out_ref[...] = (cent_ref[...].astype(F32) + sums) / mass_scr[:, 0:1]


def level2(place, back, pieces, centroids2):
    rows = centroids2.shape[0]
    subs = len(pieces)
    width = 256
    return pl.pallas_call(
        level2_kernel,
        grid_spec=pltpu.PrefetchScalarGridSpec(
            num_scalar_prefetch=1,
            grid=(D // width,),
            in_specs=[
                pl.BlockSpec(
                    (subs, BLK, 128), lambda i, place: (place[4], 0, (CAP * D + TILE) // 128)
                ),
                pl.BlockSpec((rows, width), lambda i, place: (0, i)),
            ]
            + [ANY] * subs,
            out_specs=pl.BlockSpec((rows, width), lambda i, place: (0, i)),
            scratch_shapes=[
                pltpu.VMEM((subs * CAP2, D), BF),
                pltpu.VMEM((rows, subs * CAP2), BF),
                pltpu.VMEM((subs, CAP2), F32),
                pltpu.VMEM((subs, CAP2), F32),
                pltpu.VMEM((rows, 128), F32),
                pltpu.SemaphoreType.DMA,
            ],
        ),
        out_shape=jax.ShapeDtypeStruct((rows, D), F32),
        name="level2",
    )(place, back, centroids2, *pieces)


def level1_kernel(
    asked, order, start, back_ref, cent_ref, out_ref,
    back_scr, cent_scr, mass_scr, stage, sem_back, sem_cent, sem_out,
):
    parts = cent_scr.shape[0]
    part = cent_scr.shape[1]
    lane = iota((BLK, 128), 1)
    back = pltpu.make_async_copy(back_ref, back_scr, sem_back)
    back.start()

    def cents(g):
        return pltpu.make_async_copy(
            cent_ref.at[pl.ds(g * part, part)], cent_scr.at[g], sem_cent.at[g]
        )

    def out(g):
        return pltpu.make_async_copy(
            stage.at[g % 2], out_ref.at[pl.ds(g * part, part)], sem_out.at[g % 2]
        )

    for g in range(parts):
        cents(g).start()
    for g in range(parts):
        k = g % 2
        if g >= 2:
            out(g - 2).wait()
        cents(g).wait()
        stage[k] = cent_scr[g].astype(F32)
        mass_scr[...] = jnp.zeros(mass_scr.shape, F32)
        if g == 0:
            back.wait()

        def add(i, carry):
            s = order[i]
            b = asked[s] - g * part
            o = s // CAP
            at = s - o * CAP
            sums = back_scr[o, :, pl.ds(pl.multiple_of(at * D, D), D)]
            stage[k, b] = stage[k, b] + sums.astype(F32)
            m = back_scr[o, :, CAP * D + TILE :].astype(F32)
            mass_scr[b] = mass_scr[b] + jnp.where(
                (lane == 2 * at) | (lane == 2 * at + 1), m, 0.0
            )
            return carry

        lax.fori_loop(start[g], start[g + 1], add, 0)
        total = jnp.sum(mass_scr[...], axis=2, keepdims=True)
        stage[k] = stage[k] * (1.0 / (1.0 + total))
        out(g).start()
    for g in range(parts - 2, parts):
        out(g).wait()


def level1(asked, order, start, back, table):
    blocks = table.shape[0]
    parts = start.shape[0] - 1
    part = blocks // parts
    return pl.pallas_call(
        level1_kernel,
        grid_spec=pltpu.PrefetchScalarGridSpec(
            num_scalar_prefetch=3,
            grid=(),
            in_specs=[ANY, ANY],
            out_specs=ANY,
            scratch_shapes=[
                pltpu.VMEM(back.shape, BF),
                pltpu.VMEM((parts, part, BLK, D), BF),
                pltpu.VMEM((part, BLK, 128), F32),
                pltpu.VMEM((2, part, BLK, D), F32),
                pltpu.SemaphoreType.DMA,
                pltpu.SemaphoreType.DMA((parts,)),
                pltpu.SemaphoreType.DMA((2,)),
            ],
        ),
        out_shape=jax.ShapeDtypeStruct((blocks, BLK, D), F32),
        name="level1",
    )(asked, order, start, back, table)


def shards(points, level1_ids, level2_ids, level3_ids, needed, centroids1, centroids2, centroids3):
    both = ("grp", "sub")
    devices = lax.axis_size(both)
    subs = lax.axis_size("sub")
    group = lax.axis_index("grp")
    sub = lax.axis_index("sub")
    me = group * subs + sub
    blocks = K1_DEV // BLK
    wide = D // TILE
    wanted = needed[0]
    need = wanted.shape[0]
    place = jnp.stack([sub, group * subs, me >> 2, me & 3, group]).astype(I32)

    def swap(values, axes):
        return lax.all_to_all(values, axes, split_axis=0, concat_axis=0, tiled=True)

    owners = wanted // blocks
    same = (owners[:, None] == owners[None, :]) & (
        jnp.arange(need)[None, :] < jnp.arange(need)[:, None]
    )
    slot = owners * CAP + jnp.sum(same.astype(I32), axis=1)
    requests = (
        jnp.sum(
            jnp.where(
                slot[:, None] == jnp.arange(devices * CAP)[None, :],
                wanted[:, None] % blocks + 1,
                0,
            ),
            axis=0,
        )
        - 1
    )
    asked = swap(requests.reshape(devices, 1, CAP), both).reshape(devices * CAP)
    pieces, slot2, aux = route(place, level2_ids, points, subs)
    asked, aux = lax.optimization_barrier((asked, aux))
    pieces = list(pieces)
    for k in range(1, subs):
        pieces[k] = lax.ppermute(pieces[k], "sub", [(i, (i + k) % subs) for i in range(subs)])
    table = centroids1.reshape(blocks, BLK, D)
    served = serve(asked, table)
    fetched = swap(served, both)
    count = devices * CAP
    key = jnp.where(asked < 0, blocks, asked) * count + jnp.arange(count)
    position = jnp.sum((key[None, :] < key[:, None]).astype(I32), axis=1)
    order = jnp.sum(
        jnp.where(position[:, None] == jnp.arange(count)[None, :], jnp.arange(count)[:, None], 0),
        axis=0,
    )
    parts = 8
    bounds = jnp.arange(parts + 1) * (blocks // parts) * count
    start = jnp.sum((key[None, :] < bounds[:, None]).astype(I32), axis=1)
    slot, order, start = lax.optimization_barrier((slot, order, start))
    sums = weigh(slot, place, fetched, level1_ids, level3_ids, slot2, aux, points, devices)
    back = swap(sums, both)
    tiles = level3(place, back, centroids3)
    tiles = swap(tiles, both)
    level2_new = level2(place, back, pieces, centroids2[0])[None]
    level1_new = level1(asked, order, start, back, table).reshape(K1_DEV, D)
    level3_new = (
        tiles.reshape(K3 // BLK, wide, BLK, TILE).transpose(0, 2, 1, 3).reshape(K3, D).astype(F32)
    )
    return level1_new, level2_new, level3_new


def solution(mesh):
    placed = (
        P(("grp", "sub"), None),
        P(("grp", "sub")),
        P(("grp", "sub")),
        P(("grp", "sub")),
        P(("grp", "sub"), None),
        P(("grp", "sub"), None),
        P("grp", "sub", None),
        P(),
    )

    return jax.shard_map(
        shards,
        mesh=mesh,
        in_specs=placed,
        out_specs=(P(("grp", "sub"), None), P("grp", "sub", None), P()),
        check_vma=False,
    )
```

time: 280 us -> 257 us (0.918)
  the two profiles are of different devices: /device:TPU:0 before, /device:TPU:33 now
where the time goes in v2:
time: 257 us; the launch traced here: 256 us
  waiting for transfers between devices  125 us (49%)
  starting transfers between devices  73.2 us (28%)
  Pallas kernels  46.9 us (18%)
  other arithmetic  5.06 us (2%)
  local copies, waits for them, and re-layouts  4.59 us (2%)
    ppermute x15, waiting for transfers between devices, shards(): lax.ppermute(pieces[k], 'sub', [(i, (i + k) % subs) for i in range(subs)])  76.3 us
    all_to_all x4, waiting for transfers between devices, swap(): return lax.all_to_all(values, axes, split_axis=0, concat_axis=0, tiled=True)  48.8 us
    all_to_all x4, starting transfers between devices, swap(): return lax.all_to_all(values, axes, split_axis=0, concat_axis=0, tiled=True)  46.2 us
    ppermute x15, starting transfers between devices, shards(): lax.ppermute(pieces[k], 'sub', [(i, (i + k) % subs) for i in range(subs)])  27 us
    pallas_call x1, Pallas kernels, weigh(): pl.pallas_call(weigh_kernel, grid_spec=pltpu.PrefetchScalarGridSpec(num_s...  11.5 us
    pallas_call x1, Pallas kernels, level1(): pl.pallas_call(level1_kernel, grid_spec=pltpu.PrefetchScalarGridSpec(num_...  10.9 us
    pallas_call x1, Pallas kernels, route(): pl.pallas_call(route_kernel, grid_spec=pltpu.PrefetchScalarGridSpec(num_s...  8.8 us
    pallas_call x1, Pallas kernels, level2(): pl.pallas_call(level2_kernel, grid_spec=pltpu.PrefetchScalarGridSpec(num_...  8.01 us
  transfers between devices with their start and end apart: 19, of which 7 were waited for; matrix products, arithmetic and copies ran while one was open for 1% of the time, Pallas kernels for 12%

profile of v2, /device:TPU:33, one launch (start us, length us, event | category | flops | bytes accessed | tf_op | source)
XLA Modules:
  0.0 255.9 jit_solution(14228235229717257989)
XLA Ops:
  2.3 0.8 sub.17
  3.1 10.5 %all-to-all-start = ((s32[128,1,2]{2,1,0:T(1,128)}), s32[128,1,2]{2,1,0:T(1,128)S(1)}, u32[]{:S(2)}, u32[]{:S(2)}) async-start(s32[128,1,2]{2,1,0:T(1,128)} %bitcast.2), calls=%async_computation | async-start | bytes 131072 | tf_op jit(solution)/shard_map/all_to_all | solution.py:435
  13.6 0.7 stack.23.place
  14.3 8.8 %route.1 = (bf16[128,1024]{1,0:T(8,128)(2,1)}, bf16[128,1024]{1,0:T(8,128)(2,1)}, bf16[128,1024]{1,0:T(8,128)(2,1)}, bf16[128,1024]{1,0:T(8,128)(2,1)}, bf16[128...) custom-call(s32[5]{0:T(128)} %stack.23.place, ...), custom_call_target="tpu_custom_call" | custom-call | tf_op jit(solution)/shard_map/route/pallas_call | solution.py:70
  23.6 0.8 reduce.3
  24.4 0.7 reshape.122.asked
  25.1 4.8 %serve.1 = bf16[256,8,1024]{2,1,0:T(8,128)(2,1)} custom-call(s32[256]{0:T(256)} %reshape.122.asked, bf16[256,8,1024]{2,1,0:T(8,128)(2,1)} %bitcast.35), custom_call_target="tpu_custom_call" | custom-call | tf_op jit(solution)/shard_map/serve/pallas_call | solution.py:98
  29.9 10.2 %all-to-all-start.1 = ((bf16[256,8,1024]{2,1,0:T(8,128)(2,1)}), bf16[256,8,1024]{2,1,0:T(8,128)(2,1)}, u32[]{:S(2)}, u32[]{:S(2)}) async-start(bf16[256,8,1024]{2,1,0:T(8,128)(2,1)} %serve.1), calls=%async_computation.1 | async-start | bytes 8388608 | tf_op jit(solution)/shard_map/all_to_all | solution.py:435
  40.2 0.7 convert_reduce_fusion.2.start
  41.7 48.8 %all-to-all-done.1.fetched_ref = bf16[256,8,1024]{2,1,0:T(8,128)(2,1)} async-done(((bf16[256,8,1024]{2,1,0:T(8,128)(2,1)}), bf16[256,8,1024]{2,1,0:T(8,128)(2,1)}, u32[]{:S(2)}, u32[]{:S(2)}) %all-to-all-start.1) | async-done | bytes 4194336 | tf_op jit(solution)/shard_map/all_to_all | solution.py:435
  90.5 1.0 broadcast_in_dim.55.col1_ref
  91.5 11.5 %weigh.1 = bf16[128,8,2432]{2,1,0:T(8,128)(2,1)} custom-call(s32[128]{0:T(128)} %copy-done.17, s32[5]{0:T(128)} %stack.23.place, bf16[256,8,1024]{2,1,0:T(8,128)(2,1)} %all-to-all-done.1.fetched_ref, s32[1024,128]{1,0:T(8,128)} %broadcast_in_dim.55.col1_ref, s32[1,1024]{1,0:T(1,128)} %bitcast.42, s32[1,1024]{1,0:T(1,128)} %bitcast.44, ...), custom_call_target="tpu_custom_call" | custom-call | tf_op jit(solution)/shard_map/weigh/pallas_call | solution.py:199
  103.2 7.0 %all-to-all-start.2 = ((bf16[128,8,2432]{2,1,0:T(8,128)(2,1)}), bf16[128,8,2432]{2,1,0:T(8,128)(2,1)}, u32[]{:S(2)}, u32[]{:S(2)}) async-start(bf16[128,8,2432]{2,1,0:T(8,128)(2,1)} %weigh.1), calls=%async_computation.2 | async-start | bytes 9961472 | tf_op jit(solution)/shard_map/all_to_all | solution.py:435
  110.2 1.3 collective-permute-start
  111.5 2.5 collective-permute-start.1
  114.0 2.4 collective-permute-start.10
  116.4 2.6 %collective-permute-start.11 = (bf16[128,1024]{1,0:T(8,128)(2,1)S(1)}, bf16[128,1024]{1,0:T(8,128)(2,1)S(1)}, u32[]{:S(2)}, u32[]{:S(2)}) collective-permute-start(bf16[128,1024]{1,0:T(8,128)(2,1)S(1)} %copy-done.22), channel_id=1, source_target_pairs={{0,12},{1,13},{2,14},{3,15},{4,0},{5,1},{6,2},{7,3},{8,4},{9,5},{1... | collective-permute-start | bytes 786440 | tf_op jit(solution)/shard_map/ppermute | solution.py:458
  119.0 54.0 %collective-permute-done.refs_1_ = bf16[128,1024]{1,0:T(8,128)(2,1)S(1)} collective-permute-done((bf16[128,1024]{1,0:T(8,128)(2,1)S(1)}, bf16[128,1024]{1,0:T(8,128)(2,1)S(1)}, u32[]{:S(2)}, u32[]{:S(2)}) %collective-permute-start) | collective-permute-done | bytes 262176 | tf_op jit(solution)/shard_map/ppermute | solution.py:458
  173.3 4.6 %collective-permute-done.1.refs_2_ = bf16[128,1024]{1,0:T(8,128)(2,1)S(1)} collective-permute-done((bf16[128,1024]{1,0:T(8,128)(2,1)S(1)}, bf16[128,1024]{1,0:T(8,128)(2,1)S(1)}, u32[]{:S(2)}, u32[]{:S(2)}) %collective-permute-start.1) | collective-permute-done | bytes 262176 | tf_op jit(solution)/shard_map/ppermute | solution.py:458
  178.0 4.5 %collective-permute-start.2 = (bf16[128,1024]{1,0:T(8,128)(2,1)}, bf16[128,1024]{1,0:T(8,128)(2,1)S(1)}, u32[]{:S(2)}, u32[]{:S(2)}) collective-permute-start(bf16[128,1024]{1,0:T(8,128)(2,1)} %get-tuple-element.36), channel_id=1, source_target_pairs={{0,3},{1,4},{2,5},{3,6},{4,7},{5,8},{6,9},{7,10},{8,11},{9,12},{10... | collective-permute-start | bytes 786440 | tf_op jit(solution)/shard_map/ppermute | solution.py:458
  183.2 1.6 collective-permute-start.4
  184.8 2.8 %level3.1 = bf16[128,8,256]{2,1,0:T(8,128)(2,1)} custom-call(s32[5]{0:T(128)} %stack.23.place, bf16[128,8,2432]{2,1,0:T(8,128)(2,1)} %all-to-all-done.2.back_ref.ext_ref.tile_ref, bf16[128,8,2432]{2,1,0:T(8,128)(2,1)} %all-to-all-done.2.back_ref.ext_ref.tile_ref, bf16[256,1024]{1,0:T(8,128)(2,1)} %cent_ref.1), custom_call_target="tpu_custom_call" | custom-call | tf_op jit(solution)/shard_map/level3/pallas_call | solution.py:250
  187.7 18.5 %all-to-all-start.3 = ((bf16[128,8,256]{2,1,0:T(8,128)(2,1)}), bf16[128,8,256]{2,1,0:T(8,128)(2,1)S(1)}, u32[]{:S(2)}, u32[]{:S(2)}) async-start(bf16[128,8,256]{2,1,0:T(8,128)(2,1)} %level3.1), calls=%async_computation.3 | async-start | bytes 1048576 | tf_op jit(solution)/shard_map/all_to_all | solution.py:435
  206.2 4.1 %collective-permute-start.5 = (bf16[128,1024]{1,0:T(8,128)(2,1)}, bf16[128,1024]{1,0:T(8,128)(2,1)S(1)}, u32[]{:S(2)}, u32[]{:S(2)}) collective-permute-start(bf16[128,1024]{1,0:T(8,128)(2,1)} %get-tuple-element.39), channel_id=1, source_target_pairs={{0,6},{1,7},{2,8},{3,9},{4,10},{5,11},{6,12},{7,13},{8,14},{9,15},... | collective-permute-start | bytes 786440 | tf_op jit(solution)/shard_map/ppermute | solution.py:458
  210.6 3.8 %collective-permute-start.7 = (bf16[128,1024]{1,0:T(8,128)(2,1)}, bf16[128,1024]{1,0:T(8,128)(2,1)S(1)}, u32[]{:S(2)}, u32[]{:S(2)}) collective-permute-start(bf16[128,1024]{1,0:T(8,128)(2,1)} %get-tuple-element.41), channel_id=1, source_target_pairs={{0,8},{1,9},{2,10},{3,11},{4,12},{5,13},{6,14},{7,15},{8,0},{9,1},... | collective-permute-start | bytes 786440 | tf_op jit(solution)/shard_map/ppermute | solution.py:458
  214.5 3.4 %collective-permute-start.9 = (bf16[128,1024]{1,0:T(8,128)(2,1)S(1)}, bf16[128,1024]{1,0:T(8,128)(2,1)S(1)}, u32[]{:S(2)}, u32[]{:S(2)}) collective-permute-start(bf16[128,1024]{1,0:T(8,128)(2,1)S(1)} %copy-done.18), channel_id=1, source_target_pairs={{0,10},{1,11},{2,12},{3,13},{4,14},{5,15},{6,0},{7,1},{8,2},{9,3},... | collective-permute-start | bytes 786440 | tf_op jit(solution)/shard_map/ppermute | solution.py:458
  217.9 10.9 %level1.1 = f32[256,8,1024]{2,1,0:T(8,128)} custom-call(s32[256]{0:T(256)} %reshape.122.asked, s32[256]{0:T(256)} %select_reduce_fusion.order, s32[9]{0:T(128)} %convert_reduce_fusion.2.start, bf16[128,8,2432]{2,1,0:T(8,128)(2,1)} %all-to-all-done.2.back_ref.ext_ref.tile_ref, bf16[256,8,1024]{2,1,0:T(8,128)(2,1)} %bitcast.36), custom_call_target="tpu_custom_call" | custom-call | tf_op jit(solution)/shard_map/level1/pallas_call | solution.py:399
  228.9 6.6 %collective-permute-done.6.refs_7_ = bf16[128,1024]{1,0:T(8,128)(2,1)S(1)} collective-permute-done((bf16[128,1024]{1,0:T(8,128)(2,1)}, bf16[128,1024]{1,0:T(8,128)(2,1)S(1)}, u32[]{:S(2)}, u32[]{:S(2)}) %collective-permute-start.6) | collective-permute-done | bytes 262176 | tf_op jit(solution)/shard_map/ppermute | solution.py:458
  235.5 10.4 %collective-permute-done.7.refs_8_ = bf16[128,1024]{1,0:T(8,128)(2,1)S(1)} collective-permute-done((bf16[128,1024]{1,0:T(8,128)(2,1)}, bf16[128,1024]{1,0:T(8,128)(2,1)S(1)}, u32[]{:S(2)}, u32[]{:S(2)}) %collective-permute-start.7) | collective-permute-done | bytes 262176 | tf_op jit(solution)/shard_map/ppermute | solution.py:458
  245.9 0.7 copy-done.12
  246.8 8.0 %level2.1 = f32[512,1024]{1,0:T(8,128)} custom-call(s32[5]{0:T(128)} %stack.23.place, bf16[128,8,2432]{2,1,0:T(8,128)(2,1)} %all-to-all-done.2.back_ref.ext_ref.tile_ref, bf16[512,1024]{1,0:T(8,128)(2,1)} %bitcast.40, bf16[128,1024]{1,0:T(8,128)(2,1)} %get-tuple-element.33.refs_0_, bf16[128,1024]{1,0:T(8,128)(2,1)} %copy-done, bf16[128,1024]{1,0:T(8,128)(2,1)} %copy-done.1, ...), custom_call_target="tpu_custom_call" | custom-call | tf_op jit(solution)/shard_map/level2/pallas_call | solution.py:315
  254.8 1.1 convert.3
  (82 shorter events, 4.8 us)
Async XLA Ops:
  2.1 27.8 %copy-start.17 = (s32[128]{0:T(128)}, s32[128]{0:T(128)S(1)}, u32[]{:S(2)}) copy-start(s32[128]{0:T(128)S(1)} %multiply_add_fusion.slot) | copy-start | bytes 1540
  3.1 20.0 %all-to-all-start = ((s32[128,1,2]{2,1,0:T(1,128)}), s32[128,1,2]{2,1,0:T(1,128)S(1)}, u32[]{:S(2)}, u32[]{:S(2)}) async-start(s32[128,1,2]{2,1,0:T(1,128)} %bitcast.2), calls=%async_computation | async-start | bytes 131072 | tf_op jit(solution)/shard_map/all_to_all | solution.py:435
  29.9 60.6 %copy-start.15 = (s32[1024]{0:T(1024)S(1)}, s32[1024]{0:T(1024)}, u32[]{:S(2)}) copy-start(s32[1024]{0:T(1024)} %param.9) | copy-start | bytes 12292
  29.9 60.6 %all-to-all-start.1 = ((bf16[256,8,1024]{2,1,0:T(8,128)(2,1)}), bf16[256,8,1024]{2,1,0:T(8,128)(2,1)}, u32[]{:S(2)}, u32[]{:S(2)}) async-start(bf16[256,8,1024]{2,1,0:T(8,128)(2,1)} %serve.1), calls=%async_computation.1 | async-start | bytes 8388608 | tf_op jit(solution)/shard_map/all_to_all | solution.py:435
  103.1 15.9 %copy-start.21 = (bf16[128,1024]{1,0:T(8,128)(2,1)S(1)}, bf16[128,1024]{1,0:T(8,128)(2,1)}, u32[]{:S(2)}) copy-start(bf16[128,1024]{1,0:T(8,128)(2,1)} %get-tuple-element.46) | copy-start | bytes 786436
  103.1 79.4 %copy-start.20 = (bf16[128,1024]{1,0:T(8,128)(2,1)S(1)}, bf16[128,1024]{1,0:T(8,128)(2,1)}, u32[]{:S(2)}) copy-start(bf16[128,1024]{1,0:T(8,128)(2,1)} %get-tuple-element.37) | copy-start | bytes 786436
  103.2 80.1 %copy-start.19 = (bf16[128,1024]{1,0:T(8,128)(2,1)S(1)}, bf16[128,1024]{1,0:T(8,128)(2,1)}, u32[]{:S(2)}) copy-start(bf16[128,1024]{1,0:T(8,128)(2,1)} %get-tuple-element.38) | copy-start | bytes 786436
  103.2 81.6 %all-to-all-start.2 = ((bf16[128,8,2432]{2,1,0:T(8,128)(2,1)}), bf16[128,8,2432]{2,1,0:T(8,128)(2,1)}, u32[]{:S(2)}, u32[]{:S(2)}) async-start(bf16[128,8,2432]{2,1,0:T(8,128)(2,1)} %weigh.1), calls=%async_computation.2 | async-start | bytes 9961472 | tf_op jit(solution)/shard_map/all_to_all | solution.py:435
  110.2 62.8 %collective-permute-start = (bf16[128,1024]{1,0:T(8,128)(2,1)S(1)}, bf16[128,1024]{1,0:T(8,128)(2,1)S(1)}, u32[]{:S(2)}, u32[]{:S(2)}) collective-permute-start(bf16[128,1024]{1,0:T(8,128)(2,1)S(1)} %copy-done.25), channel_id=1, source_target_pairs={{0,1},{1,2},{2,3},{3,4},{4,5},{5,6},{6,7},{7,8},{8,9},{9,10},{10,1... | collective-permute-start | bytes 786440 | tf_op jit(solution)/shard_map/ppermute | solution.py:458
  111.5 66.4 %collective-permute-start.1 = (bf16[128,1024]{1,0:T(8,128)(2,1)S(1)}, bf16[128,1024]{1,0:T(8,128)(2,1)S(1)}, u32[]{:S(2)}, u32[]{:S(2)}) collective-permute-start(bf16[128,1024]{1,0:T(8,128)(2,1)S(1)} %copy-done.24), channel_id=1, source_target_pairs={{0,2},{1,3},{2,4},{3,5},{4,6},{5,7},{6,8},{7,9},{8,10},{9,11},{10,... | collective-permute-start | bytes 786440 | tf_op jit(solution)/shard_map/ppermute | solution.py:458
  114.0 63.9 %collective-permute-start.10 = (bf16[128,1024]{1,0:T(8,128)(2,1)S(1)}, bf16[128,1024]{1,0:T(8,128)(2,1)S(1)}, u32[]{:S(2)}, u32[]{:S(2)}) collective-permute-start(bf16[128,1024]{1,0:T(8,128)(2,1)S(1)} %copy-done.23), channel_id=1, source_target_pairs={{0,11},{1,12},{2,13},{3,14},{4,15},{5,0},{6,1},{7,2},{8,3},{9,4},{... | collective-permute-start | bytes 786440 | tf_op jit(solution)/shard_map/ppermute | solution.py:458
  116.4 66.1 %collective-permute-start.11 = (bf16[128,1024]{1,0:T(8,128)(2,1)S(1)}, bf16[128,1024]{1,0:T(8,128)(2,1)S(1)}, u32[]{:S(2)}, u32[]{:S(2)}) collective-permute-start(bf16[128,1024]{1,0:T(8,128)(2,1)S(1)} %copy-done.22), channel_id=1, source_target_pairs={{0,12},{1,13},{2,14},{3,15},{4,0},{5,1},{6,2},{7,3},{8,4},{9,5},{1... | collective-permute-start | bytes 786440 | tf_op jit(solution)/shard_map/ppermute | solution.py:458
  119.0 64.2 %collective-permute-start.12 = (bf16[128,1024]{1,0:T(8,128)(2,1)S(1)}, bf16[128,1024]{1,0:T(8,128)(2,1)S(1)}, u32[]{:S(2)}, u32[]{:S(2)}) collective-permute-start(bf16[128,1024]{1,0:T(8,128)(2,1)S(1)} %copy-done.21), channel_id=1, source_target_pairs={{0,13},{1,14},{2,15},{3,0},{4,1},{5,2},{6,3},{7,4},{8,5},{9,6},{10... | collective-permute-start | bytes 786440 | tf_op jit(solution)/shard_map/ppermute | solution.py:458
  173.0 14.7 %copy-start = (bf16[128,1024]{1,0:T(8,128)(2,1)}, bf16[128,1024]{1,0:T(8,128)(2,1)S(1)}, u32[]{:S(2)}) copy-start(bf16[128,1024]{1,0:T(8,128)(2,1)S(1)} %collective-permute-done.refs_1_) | copy-start | bytes 786436
  173.0 33.2 %collective-permute-start.13 = (bf16[128,1024]{1,0:T(8,128)(2,1)}, bf16[128,1024]{1,0:T(8,128)(2,1)S(1)}, u32[]{:S(2)}, u32[]{:S(2)}) collective-permute-start(bf16[128,1024]{1,0:T(8,128)(2,1)} %get-tuple-element.47), channel_id=1, source_target_pairs={{0,14},{1,15},{2,0},{3,1},{4,2},{5,3},{6,4},{7,5},{8,6},{9,7},{10,... | collective-permute-start | bytes 786440 | tf_op jit(solution)/shard_map/ppermute | solution.py:458
  177.9 32.4 %collective-permute-start.14 = (bf16[128,1024]{1,0:T(8,128)(2,1)}, bf16[128,1024]{1,0:T(8,128)(2,1)S(1)}, u32[]{:S(2)}, u32[]{:S(2)}) collective-permute-start(bf16[128,1024]{1,0:T(8,128)(2,1)} %get-tuple-element.48), channel_id=1, source_target_pairs={{0,15},{1,0},{2,1},{3,2},{4,3},{5,4},{6,5},{7,6},{8,7},{9,8},{10,9... | collective-permute-start | bytes 786440 | tf_op jit(solution)/shard_map/ppermute | solution.py:458
  178.0 32.7 %collective-permute-start.2 = (bf16[128,1024]{1,0:T(8,128)(2,1)}, bf16[128,1024]{1,0:T(8,128)(2,1)S(1)}, u32[]{:S(2)}, u32[]{:S(2)}) collective-permute-start(bf16[128,1024]{1,0:T(8,128)(2,1)} %get-tuple-element.36), channel_id=1, source_target_pairs={{0,3},{1,4},{2,5},{3,6},{4,7},{5,8},{6,9},{7,10},{8,11},{9,12},{10... | collective-permute-start | bytes 786440 | tf_op jit(solution)/shard_map/ppermute | solution.py:458
  182.5 31.9 %collective-permute-start.3 = (bf16[128,1024]{1,0:T(8,128)(2,1)S(1)}, bf16[128,1024]{1,0:T(8,128)(2,1)S(1)}, u32[]{:S(2)}, u32[]{:S(2)}) collective-permute-start(bf16[128,1024]{1,0:T(8,128)(2,1)S(1)} %copy-done.20), channel_id=1, source_target_pairs={{0,4},{1,5},{2,6},{3,7},{4,8},{5,9},{6,10},{7,11},{8,12},{9,13},{1... | collective-permute-start | bytes 786440 | tf_op jit(solution)/shard_map/ppermute | solution.py:458
  183.2 31.3 %copy-start.18 = (bf16[128,1024]{1,0:T(8,128)(2,1)S(1)}, bf16[128,1024]{1,0:T(8,128)(2,1)}, u32[]{:S(2)}) copy-start(bf16[128,1024]{1,0:T(8,128)(2,1)} %get-tuple-element.43) | copy-start | bytes 786436
  183.2 31.3 %collective-permute-start.4 = (bf16[128,1024]{1,0:T(8,128)(2,1)S(1)}, bf16[128,1024]{1,0:T(8,128)(2,1)S(1)}, u32[]{:S(2)}, u32[]{:S(2)}) collective-permute-start(bf16[128,1024]{1,0:T(8,128)(2,1)S(1)} %copy-done.19), channel_id=1, source_target_pairs={{0,5},{1,6},{2,7},{3,8},{4,9},{5,10},{6,11},{7,12},{8,13},{9,14},{... | collective-permute-start | bytes 786440 | tf_op jit(solution)/shard_map/ppermute | solution.py:458
  187.7 67.1 %all-to-all-start.3 = ((bf16[128,8,256]{2,1,0:T(8,128)(2,1)}), bf16[128,8,256]{2,1,0:T(8,128)(2,1)S(1)}, u32[]{:S(2)}, u32[]{:S(2)}) async-start(bf16[128,8,256]{2,1,0:T(8,128)(2,1)} %level3.1), calls=%async_computation.3 | async-start | bytes 1048576 | tf_op jit(solution)/shard_map/all_to_all | solution.py:435
  206.2 22.6 %copy-start.5 = (bf16[128,1024]{1,0:T(8,128)(2,1)}, bf16[128,1024]{1,0:T(8,128)(2,1)S(1)}, u32[]{:S(2)}) copy-start(bf16[128,1024]{1,0:T(8,128)(2,1)S(1)} %collective-permute-done.13.refs_14_) | copy-start | bytes 786436
  206.2 22.7 %collective-permute-start.5 = (bf16[128,1024]{1,0:T(8,128)(2,1)}, bf16[128,1024]{1,0:T(8,128)(2,1)S(1)}, u32[]{:S(2)}, u32[]{:S(2)}) collective-permute-start(bf16[128,1024]{1,0:T(8,128)(2,1)} %get-tuple-element.39), channel_id=1, source_target_pairs={{0,6},{1,7},{2,8},{3,9},{4,10},{5,11},{6,12},{7,13},{8,14},{9,15},... | collective-permute-start | bytes 786440 | tf_op jit(solution)/shard_map/ppermute | solution.py:458
  210.3 18.6 %copy-start.6 = (bf16[128,1024]{1,0:T(8,128)(2,1)}, bf16[128,1024]{1,0:T(8,128)(2,1)S(1)}, u32[]{:S(2)}) copy-start(bf16[128,1024]{1,0:T(8,128)(2,1)S(1)} %collective-permute-done.14.refs_15_) | copy-start | bytes 786436
  210.3 25.2 %collective-permute-start.6 = (bf16[128,1024]{1,0:T(8,128)(2,1)}, bf16[128,1024]{1,0:T(8,128)(2,1)S(1)}, u32[]{:S(2)}, u32[]{:S(2)}) collective-permute-start(bf16[128,1024]{1,0:T(8,128)(2,1)} %get-tuple-element.40), channel_id=1, source_target_pairs={{0,7},{1,8},{2,9},{3,10},{4,11},{5,12},{6,13},{7,14},{8,15},{9,0},... | collective-permute-start | bytes 786440 | tf_op jit(solution)/shard_map/ppermute | solution.py:458
  210.6 18.2 %copy-start.7 = (bf16[128,1024]{1,0:T(8,128)(2,1)}, bf16[128,1024]{1,0:T(8,128)(2,1)S(1)}, u32[]{:S(2)}) copy-start(bf16[128,1024]{1,0:T(8,128)(2,1)S(1)} %collective-permute-done.2.refs_3_) | copy-start | bytes 786436
  210.6 35.3 %collective-permute-start.7 = (bf16[128,1024]{1,0:T(8,128)(2,1)}, bf16[128,1024]{1,0:T(8,128)(2,1)S(1)}, u32[]{:S(2)}, u32[]{:S(2)}) collective-permute-start(bf16[128,1024]{1,0:T(8,128)(2,1)} %get-tuple-element.41), channel_id=1, source_target_pairs={{0,8},{1,9},{2,10},{3,11},{4,12},{5,13},{6,14},{7,15},{8,0},{9,1},... | collective-permute-start | bytes 786440 | tf_op jit(solution)/shard_map/ppermute | solution.py:458
  214.4 14.5 %copy-start.8 = (bf16[128,1024]{1,0:T(8,128)(2,1)}, bf16[128,1024]{1,0:T(8,128)(2,1)S(1)}, u32[]{:S(2)}) copy-start(bf16[128,1024]{1,0:T(8,128)(2,1)S(1)} %collective-permute-done.3.refs_4_) | copy-start | bytes 786436
  214.4 31.5 %collective-permute-start.8 = (bf16[128,1024]{1,0:T(8,128)(2,1)}, bf16[128,1024]{1,0:T(8,128)(2,1)S(1)}, u32[]{:S(2)}, u32[]{:S(2)}) collective-permute-start(bf16[128,1024]{1,0:T(8,128)(2,1)} %get-tuple-element.42), channel_id=1, source_target_pairs={{0,9},{1,10},{2,11},{3,12},{4,13},{5,14},{6,15},{7,0},{8,1},{9,2},... | collective-permute-start | bytes 786440 | tf_op jit(solution)/shard_map/ppermute | solution.py:458
  214.5 14.4 %copy-start.9 = (bf16[128,1024]{1,0:T(8,128)(2,1)}, bf16[128,1024]{1,0:T(8,128)(2,1)S(1)}, u32[]{:S(2)}) copy-start(bf16[128,1024]{1,0:T(8,128)(2,1)S(1)} %collective-permute-done.4.refs_5_) | copy-start | bytes 786436
  214.5 31.4 %collective-permute-start.9 = (bf16[128,1024]{1,0:T(8,128)(2,1)S(1)}, bf16[128,1024]{1,0:T(8,128)(2,1)S(1)}, u32[]{:S(2)}, u32[]{:S(2)}) collective-permute-start(bf16[128,1024]{1,0:T(8,128)(2,1)S(1)} %copy-done.18), channel_id=1, source_target_pairs={{0,10},{1,11},{2,12},{3,13},{4,14},{5,15},{6,0},{7,1},{8,2},{9,3},... | collective-permute-start | bytes 786440 | tf_op jit(solution)/shard_map/ppermute | solution.py:458
  228.9 17.0 %copy-start.10 = (bf16[128,1024]{1,0:T(8,128)(2,1)}, bf16[128,1024]{1,0:T(8,128)(2,1)S(1)}, u32[]{:S(2)}) copy-start(bf16[128,1024]{1,0:T(8,128)(2,1)S(1)} %collective-permute-done.5.refs_6_) | copy-start | bytes 786436
  (13 other events, 91.9 us)

commit v3 on v2

--- a/solution.py
+++ b/solution.py
@@ -87,10 +87,12 @@
     count = out_ref.shape[0]
 
     def one(i, carry):
-        pltpu.make_async_copy(table_ref.at[jnp.maximum(asked[i], 0)], out_ref.at[i], sem).start()
+        for k in range(CAP):
+            block = jnp.maximum(asked[i, k], 0)
+            pltpu.make_async_copy(table_ref.at[block], out_ref.at[CAP * i + k], sem).start()
         return carry
 
-    lax.fori_loop(0, count, one, 0, unroll=8)
+    lax.fori_loop(0, count // CAP, one, 0, unroll=8)
     pltpu.make_async_copy(out_ref, out_ref, sem).wait()
 
 
@@ -104,7 +106,7 @@
             out_specs=ANY,
             scratch_shapes=[pltpu.SemaphoreType.DMA],
         ),
-        out_shape=jax.ShapeDtypeStruct((asked.shape[0], BLK, D), BF),
+        out_shape=jax.ShapeDtypeStruct((asked.shape[0] * CAP, BLK, D), BF),
         name="serve",
     )(asked, table)
 
@@ -236,7 +238,9 @@
     )
 
 
-def level3_kernel(place, tile_ref, ext_ref, cent_ref, out_ref):
+def level3_kernel(place, tile_ref, ext_ref, cent_ref, out_ref, own_ref):
+    subs = own_ref.shape[0]
+    own_ref[...] = ext_ref[pl.ds(pl.multiple_of(place[1], subs), subs)]
     total = jnp.sum(tile_ref[...].astype(F32), axis=0)
     ext = jnp.sum(ext_ref[...].astype(F32), axis=0)
     lane = iota((BLK, 128), 1)
@@ -245,7 +249,7 @@
     out_ref[...] = jnp.broadcast_to(new.astype(BF)[None], out_ref.shape)
 
 
-def level3(place, back, centroids3):
+def level3(place, back, centroids3, subs):
     devices = back.shape[0]
     return pl.pallas_call(
         level3_kernel,
@@ -257,9 +261,12 @@
                 pl.BlockSpec((devices, BLK, 128), lambda i, place: (0, 0, (CAP * D + TILE) // 128)),
                 pl.BlockSpec((BLK, TILE), lambda i, place: (place[2], place[3])),
             ],
-            out_specs=full((devices, BLK, TILE)),
+            out_specs=[full((devices, BLK, TILE)), full((subs, BLK, 128))],
         ),
-        out_shape=jax.ShapeDtypeStruct((devices, BLK, TILE), BF),
+        out_shape=[
+            jax.ShapeDtypeStruct((devices, BLK, TILE), BF),
+            jax.ShapeDtypeStruct((subs, BLK, 128), BF),
+        ],
         name="level3",
     )(place, back, back, centroids3)
 
@@ -308,7 +315,7 @@
     out_ref[...] = (cent_ref[...].astype(F32) + sums) / mass_scr[:, 0:1]
 
 
-def level2(place, back, pieces, centroids2):
+def level2(place, ext, pieces, centroids2):
     rows = centroids2.shape[0]
     subs = len(pieces)
     width = 256
@@ -318,9 +325,7 @@
             num_scalar_prefetch=1,
             grid=(D // width,),
             in_specs=[
-                pl.BlockSpec(
-                    (subs, BLK, 128), lambda i, place: (place[4], 0, (CAP * D + TILE) // 128)
-                ),
+                full(ext.shape),
                 pl.BlockSpec((rows, width), lambda i, place: (0, i)),
             ]
             + [ANY] * subs,
@@ -335,16 +340,18 @@
             ],
         ),
         out_shape=jax.ShapeDtypeStruct((rows, D), F32),
+        compiler_params=pltpu.CompilerParams(vmem_limit_bytes=24 << 20),
         name="level2",
-    )(place, back, centroids2, *pieces)
+    )(place, ext, centroids2, *pieces)
 
 
 def level1_kernel(
-    asked, order, start, back_ref, cent_ref, out_ref,
+    order, start, back_ref, cent_ref, out_ref,
     back_scr, cent_scr, mass_scr, stage, sem_back, sem_cent, sem_out,
 ):
     parts = cent_scr.shape[0]
     part = cent_scr.shape[1]
+    slots = CAP * back_scr.shape[0]
     lane = iota((BLK, 128), 1)
     back = pltpu.make_async_copy(back_ref, back_scr, sem_back)
     back.start()
@@ -371,20 +378,33 @@
         if g == 0:
             back.wait()
 
+        first, last = start[g], start[g + 1]
+
         def add(i, carry):
-            s = order[i]
-            b = asked[s] - g * part
-            o = s // CAP
-            at = s - o * CAP
-            sums = back_scr[o, :, pl.ds(pl.multiple_of(at * D, D), D)]
-            stage[k, b] = stage[k, b] + sums.astype(F32)
-            m = back_scr[o, :, CAP * D + TILE :].astype(F32)
-            mass_scr[b] = mass_scr[b] + jnp.where(
-                (lane == 2 * at) | (lane == 2 * at + 1), m, 0.0
-            )
+            loaded = []
+            for j in range(4):
+                at = first + 4 * i + j
+                valid = at < last
+                code = order[jnp.minimum(at, last - 1)]
+                s = code % slots
+                o = s // CAP
+                side = s - o * CAP
+                sums = back_scr[o, :, pl.ds(pl.multiple_of(side * D, D), D)].astype(F32)
+                m = back_scr[o, :, CAP * D + TILE :].astype(F32)
+                mine = (lane == 2 * side) | (lane == 2 * side + 1)
+                loaded.append(
+                    (
+                        code // slots - g * part,
+                        jnp.where(valid, sums, 0.0),
+                        jnp.where(mine & valid, m, 0.0),
+                    )
+                )
+            for b, sums, m in loaded:
+                stage[k, b] = stage[k, b] + sums
+                mass_scr[b] = mass_scr[b] + m
             return carry
 
-        lax.fori_loop(start[g], start[g + 1], add, 0)
+        lax.fori_loop(0, (last - first + 3) // 4, add, 0)
         total = jnp.sum(mass_scr[...], axis=2, keepdims=True)
         stage[k] = stage[k] * (1.0 / (1.0 + total))
         out(g).start()
@@ -392,14 +412,14 @@
         out(g).wait()
 
 
-def level1(asked, order, start, back, table):
+def level1(order, start, back, table):
     blocks = table.shape[0]
     parts = start.shape[0] - 1
     part = blocks // parts
     return pl.pallas_call(
         level1_kernel,
         grid_spec=pltpu.PrefetchScalarGridSpec(
-            num_scalar_prefetch=3,
+            num_scalar_prefetch=2,
             grid=(),
             in_specs=[ANY, ANY],
             out_specs=ANY,
@@ -415,7 +435,7 @@
         ),
         out_shape=jax.ShapeDtypeStruct((blocks, BLK, D), F32),
         name="level1",
-    )(asked, order, start, back, table)
+    )(order, start, back, table)
 
 
 def shards(points, level1_ids, level2_ids, level3_ids, needed, centroids1, centroids2, centroids3):
@@ -450,7 +470,8 @@
         )
         - 1
     )
-    asked = swap(requests.reshape(devices, 1, CAP), both).reshape(devices * CAP)
+    requests = jnp.pad(requests.reshape(devices, 1, CAP), ((0, 0), (0, 0), (0, 128 - CAP)))
+    asked = swap(requests, both).reshape(devices, 128)
     pieces, slot2, aux = route(place, level2_ids, points, subs)
     asked, aux = lax.optimization_barrier((asked, aux))
     pieces = list(pieces)
@@ -460,11 +481,11 @@
     served = serve(asked, table)
     fetched = swap(served, both)
     count = devices * CAP
-    key = jnp.where(asked < 0, blocks, asked) * count + jnp.arange(count)
+    flat = asked[:, :CAP].reshape(count)
+    key = jnp.where(flat < 0, blocks, flat) * count + jnp.arange(count)
     position = jnp.sum((key[None, :] < key[:, None]).astype(I32), axis=1)
     order = jnp.sum(
-        jnp.where(position[:, None] == jnp.arange(count)[None, :], jnp.arange(count)[:, None], 0),
-        axis=0,
+        jnp.where(position[:, None] == jnp.arange(count)[None, :], key[:, None], 0), axis=0
     )
     parts = 8
     bounds = jnp.arange(parts + 1) * (blocks // parts) * count
@@ -472,10 +493,10 @@
     slot, order, start = lax.optimization_barrier((slot, order, start))
     sums = weigh(slot, place, fetched, level1_ids, level3_ids, slot2, aux, points, devices)
     back = swap(sums, both)
-    tiles = level3(place, back, centroids3)
+    tiles, ext = level3(place, back, centroids3, subs)
     tiles = swap(tiles, both)
-    level2_new = level2(place, back, pieces, centroids2[0])[None]
-    level1_new = level1(asked, order, start, back, table).reshape(K1_DEV, D)
+    level2_new = level2(place, ext, pieces, centroids2[0])[None]
+    level1_new = level1(order, start, back, table).reshape(K1_DEV, D)
     level3_new = (
         tiles.reshape(K3 // BLK, wide, BLK, TILE).transpose(0, 2, 1, 3).reshape(K3, D).astype(F32)
     )

time: 257 us -> 257 us (level)
    unnamed x52 -> x40, local copies, waits for them, and re-layouts: 0.95 us -> 4.01 us
  transfers between devices with their start and end apart: 19 -> 19, of which waited for: 7 -> 7; matrix products, arithmetic and copies ran while one was open for 1% -> 1% of each run, Pallas kernels for 12% -> 11%
where the time goes in v3:
time: 257 us; the launch traced here: 256 us
  waiting for transfers between devices  123 us (48%)
  starting transfers between devices  73.6 us (29%)
  Pallas kernels  46.1 us (18%)
  local copies, waits for them, and re-layouts  6.57 us (3%)
  other arithmetic  5.36 us (2%)
    ppermute x15, waiting for transfers between devices, shards(): lax.ppermute(pieces[k], 'sub', [(i, (i + k) % subs) for i in range(subs)])  74.8 us
    all_to_all x4, waiting for transfers between devices, swap(): return lax.all_to_all(values, axes, split_axis=0, concat_axis=0, tiled=True)  48.6 us
    all_to_all x4, starting transfers between devices, swap(): return lax.all_to_all(values, axes, split_axis=0, concat_axis=0, tiled=True)  46.7 us
    ppermute x15, starting transfers between devices, shards(): lax.ppermute(pieces[k], 'sub', [(i, (i + k) % subs) for i in range(subs)])  26.9 us
    pallas_call x1, Pallas kernels, weigh(): pl.pallas_call(weigh_kernel, grid_spec=pltpu.PrefetchScalarGridSpec(num_s...  11.5 us
    pallas_call x1, Pallas kernels, level1(): pl.pallas_call(level1_kernel, grid_spec=pltpu.PrefetchScalarGridSpec(num_...  11 us
    pallas_call x1, Pallas kernels, route(): pl.pallas_call(route_kernel, grid_spec=pltpu.PrefetchScalarGridSpec(num_s...  8.79 us
    pallas_call x1, Pallas kernels, level2(): pl.pallas_call(level2_kernel, grid_spec=pltpu.PrefetchScalarGridSpec(num_...  6.01 us
  transfers between devices with their start and end apart: 19, of which 7 were waited for; matrix products, arithmetic and copies ran while one was open for 1% of the time, Pallas kernels for 11%

profile of v3, /device:TPU:33, one launch (start us, length us, event | category | flops | bytes accessed | tf_op | source)
XLA Modules:
  0.0 256.0 jit_solution(7727406399469266344)
XLA Ops:
  3.1 10.5 %all-to-all-start = ((s32[128,1,128]{2,1,0:T(1,128)}), s32[128,1,128]{2,1,0:T(1,128)S(1)}, u32[]{:S(2)}, u32[]{:S(2)}) async-start(s32[128,1,128]{2,1,0:T(1,128)} %bitcast.2), calls=%async_computation | async-start | bytes 131072 | tf_op jit(solution)/shard_map/all_to_all | solution.py:455
  14.2 8.8 %route.1 = (bf16[128,1024]{1,0:T(8,128)(2,1)}, bf16[128,1024]{1,0:T(8,128)(2,1)}, bf16[128,1024]{1,0:T(8,128)(2,1)}, bf16[128,1024]{1,0:T(8,128)(2,1)}, bf16[128...) custom-call(s32[5]{0:T(128)} %stack.23.place, ...), custom_call_target="tpu_custom_call" | custom-call | tf_op jit(solution)/shard_map/route/pallas_call | solution.py:70
  23.7 5.9 %serve.1 = bf16[256,8,1024]{2,1,0:T(8,128)(2,1)} custom-call(s32[128,128]{1,0:T(8,128)} %bitcast.43, bf16[256,8,1024]{2,1,0:T(8,128)(2,1)} %bitcast.38), custom_call_target="tpu_custom_call" | custom-call | tf_op jit(solution)/shard_map/serve/pallas_call | solution.py:100
  29.6 10.2 %all-to-all-start.1 = ((bf16[256,8,1024]{2,1,0:T(8,128)(2,1)}), bf16[256,8,1024]{2,1,0:T(8,128)(2,1)}, u32[]{:S(2)}, u32[]{:S(2)}) async-start(bf16[256,8,1024]{2,1,0:T(8,128)(2,1)} %serve.1), calls=%async_computation.1 | async-start | bytes 8388608 | tf_op jit(solution)/shard_map/all_to_all | solution.py:455
  40.9 0.8 select_reduce_fusion.order
  41.6 48.6 %all-to-all-done.1.fetched_ref = bf16[256,8,1024]{2,1,0:T(8,128)(2,1)} async-done(((bf16[256,8,1024]{2,1,0:T(8,128)(2,1)}), bf16[256,8,1024]{2,1,0:T(8,128)(2,1)}, u32[]{:S(2)}, u32[]{:S(2)}) %all-to-all-start.1) | async-done | bytes 4194336 | tf_op jit(solution)/shard_map/all_to_all | solution.py:455
  90.2 1.0 broadcast_in_dim.34.col1_ref
  91.2 11.5 %weigh.1 = bf16[128,8,2432]{2,1,0:T(8,128)(2,1)} custom-call(s32[128]{0:T(128)} %copy-done.11, s32[5]{0:T(128)} %stack.23.place, bf16[256,8,1024]{2,1,0:T(8,128)(2,1)} %all-to-all-done.1.fetched_ref, s32[1024,128]{1,0:T(8,128)} %broadcast_in_dim.34.col1_ref, s32[1,1024]{1,0:T(1,128)} %bitcast.45, s32[1,1024]{1,0:T(1,128)} %bitcast.47, ...), custom_call_target="tpu_custom_call" | custom-call | tf_op jit(solution)/shard_map/weigh/pallas_call | solution.py:201
  102.8 7.0 %all-to-all-start.2 = ((bf16[128,8,2432]{2,1,0:T(8,128)(2,1)}), bf16[128,8,2432]{2,1,0:T(8,128)(2,1)}, u32[]{:S(2)}, u32[]{:S(2)}) async-start(bf16[128,8,2432]{2,1,0:T(8,128)(2,1)} %weigh.1), calls=%async_computation.2 | async-start | bytes 9961472 | tf_op jit(solution)/shard_map/all_to_all | solution.py:455
  109.8 1.3 collective-permute-start
  111.2 2.5 collective-permute-start.1
  113.7 2.4 collective-permute-start.10
  116.0 2.6 %collective-permute-start.11 = (bf16[128,1024]{1,0:T(8,128)(2,1)S(1)}, bf16[128,1024]{1,0:T(8,128)(2,1)S(1)}, u32[]{:S(2)}, u32[]{:S(2)}) collective-permute-start(bf16[128,1024]{1,0:T(8,128)(2,1)S(1)} %copy-done.16), channel_id=1, source_target_pairs={{0,12},{1,13},{2,14},{3,15},{4,0},{5,1},{6,2},{7,3},{8,4},{9,5},{1... | collective-permute-start | bytes 786440 | tf_op jit(solution)/shard_map/ppermute | solution.py:479
  118.6 54.0 %collective-permute-done.refs_1_ = bf16[128,1024]{1,0:T(8,128)(2,1)S(1)} collective-permute-done((bf16[128,1024]{1,0:T(8,128)(2,1)S(1)}, bf16[128,1024]{1,0:T(8,128)(2,1)S(1)}, u32[]{:S(2)}, u32[]{:S(2)}) %collective-permute-start) | collective-permute-done | bytes 262176 | tf_op jit(solution)/shard_map/ppermute | solution.py:479
  173.0 4.6 %collective-permute-done.1.refs_2_ = bf16[128,1024]{1,0:T(8,128)(2,1)S(1)} collective-permute-done((bf16[128,1024]{1,0:T(8,128)(2,1)S(1)}, bf16[128,1024]{1,0:T(8,128)(2,1)S(1)}, u32[]{:S(2)}, u32[]{:S(2)}) %collective-permute-start.1) | collective-permute-done | bytes 262176 | tf_op jit(solution)/shard_map/ppermute | solution.py:479
  177.6 4.5 %collective-permute-start.2 = (bf16[128,1024]{1,0:T(8,128)(2,1)S(1)}, bf16[128,1024]{1,0:T(8,128)(2,1)S(1)}, u32[]{:S(2)}, u32[]{:S(2)}) collective-permute-start(bf16[128,1024]{1,0:T(8,128)(2,1)S(1)} %copy-done.14), channel_id=1, source_target_pairs={{0,3},{1,4},{2,5},{3,6},{4,7},{5,8},{6,9},{7,10},{8,11},{9,12},{10... | collective-permute-start | bytes 786440 | tf_op jit(solution)/shard_map/ppermute | solution.py:479
  182.2 0.7 collective-permute-done.12.refs_13_
  182.9 1.6 collective-permute-start.4
  184.4 2.9 %level3.1 = (bf16[128,8,256]{2,1,0:T(8,128)(2,1)}, bf16[16,8,128]{2,1,0:T(8,128)(2,1)}) custom-call(s32[5]{0:T(128)} %stack.23.place, bf16[128,8,2432]{2,1,0:T(8,128)(2,1)} %all-to-all-done.2.back_ref.tile_ref.ext_ref, bf16[128,8,2432]{2,1,0:T(8,128)(2,1)} %all-to-all-done.2.back_ref.tile_ref.ext_ref, bf16[256,1024]{1,0:T(8,128)(2,1)} %cent_ref.1), custom_call_target="tpu_custom_call" | custom-call | tf_op jit(solution)/shard_map/level3/pallas_call | solution.py:254
  187.3 18.9 %all-to-all-start.3 = ((bf16[128,8,256]{2,1,0:T(8,128)(2,1)}), bf16[128,8,256]{2,1,0:T(8,128)(2,1)}, u32[]{:S(2)}, u32[]{:S(2)}) async-start(bf16[128,8,256]{2,1,0:T(8,128)(2,1)} %get-tuple-element.52), calls=%async_computation.3 | async-start | bytes 1048576 | tf_op jit(solution)/shard_map/all_to_all | solution.py:455
  206.3 4.1 %collective-permute-start.5 = (bf16[128,1024]{1,0:T(8,128)(2,1)}, bf16[128,1024]{1,0:T(8,128)(2,1)}, u32[]{:S(2)}, u32[]{:S(2)}) collective-permute-start(bf16[128,1024]{1,0:T(8,128)(2,1)} %get-tuple-element.42), channel_id=1, source_target_pairs={{0,6},{1,7},{2,8},{3,9},{4,10},{5,11},{6,12},{7,13},{8,14},{9,15},... | collective-permute-start | bytes 786440 | tf_op jit(solution)/shard_map/ppermute | solution.py:479
  210.7 3.8 %collective-permute-start.7 = (bf16[128,1024]{1,0:T(8,128)(2,1)}, bf16[128,1024]{1,0:T(8,128)(2,1)}, u32[]{:S(2)}, u32[]{:S(2)}) collective-permute-start(bf16[128,1024]{1,0:T(8,128)(2,1)} %get-tuple-element.44), channel_id=1, source_target_pairs={{0,8},{1,9},{2,10},{3,11},{4,12},{5,13},{6,14},{7,15},{8,0},{9,1},... | collective-permute-start | bytes 786440 | tf_op jit(solution)/shard_map/ppermute | solution.py:479
  214.4 0.7 copy-done.2
  215.3 0.7 copy-done.4
  216.0 3.4 %collective-permute-start.9 = (bf16[128,1024]{1,0:T(8,128)(2,1)}, bf16[128,1024]{1,0:T(8,128)(2,1)}, u32[]{:S(2)}, u32[]{:S(2)}) collective-permute-start(bf16[128,1024]{1,0:T(8,128)(2,1)} %get-tuple-element.46), channel_id=1, source_target_pairs={{0,10},{1,11},{2,12},{3,13},{4,14},{5,15},{6,0},{7,1},{8,2},{9,3},... | collective-permute-start | bytes 786440 | tf_op jit(solution)/shard_map/ppermute | solution.py:479
  219.4 11.0 %level1.1 = f32[256,8,1024]{2,1,0:T(8,128)} custom-call(s32[256]{0:T(256)} %select_reduce_fusion.order, s32[9]{0:T(128)} %convert_reduce_fusion.2.start, bf16[128,8,2432]{2,1,0:T(8,128)(2,1)} %all-to-all-done.2.back_ref.tile_ref.ext_ref, bf16[256,8,1024]{2,1,0:T(8,128)(2,1)} %bitcast.39), custom_call_target="tpu_custom_call" | custom-call | tf_op jit(solution)/shard_map/level1/pallas_call | solution.py:419
  230.5 4.7 %collective-permute-done.6.refs_7_ = bf16[128,1024]{1,0:T(8,128)(2,1)} collective-permute-done((bf16[128,1024]{1,0:T(8,128)(2,1)}, bf16[128,1024]{1,0:T(8,128)(2,1)}, u32[]{:S(2)}, u32[]{:S(2)}) %collective-permute-start.6) | collective-permute-done | bytes 262176 | tf_op jit(solution)/shard_map/ppermute | solution.py:479
  235.2 10.7 %collective-permute-done.7.refs_8_ = bf16[128,1024]{1,0:T(8,128)(2,1)} collective-permute-done((bf16[128,1024]{1,0:T(8,128)(2,1)}, bf16[128,1024]{1,0:T(8,128)(2,1)}, u32[]{:S(2)}, u32[]{:S(2)}) %collective-permute-start.7) | collective-permute-done | bytes 262176 | tf_op jit(solution)/shard_map/ppermute | solution.py:479
  245.9 0.9 copy-done.3
  246.9 0.9 copy-done.5
  247.8 6.0 %level2.1 = f32[512,1024]{1,0:T(8,128)} custom-call(s32[5]{0:T(128)S(1)} %copy-done.7, bf16[16,8,128]{2,1,0:T(8,128)(2,1)S(1)} %copy-done.6, bf16[512,1024]{1,0:T(8,128)(2,1)S(1)} %bitcast.37, bf16[128,1024]{1,0:T(8,128)(2,1)S(1)} %copy-done.1, bf16[128,1024]{1,0:T(8,128)(2,1)S(1)} %collective-permute-done.refs_1_, ...), custom_call_target="tpu_custom_call" | custom-call | tf_op jit(solution)/shard_map/level2/pallas_call | solution.py:322
  253.9 2.1 convert.3
  (69 shorter events, 5.6 us)
Async XLA Ops:
  2.1 27.4 %copy-start.11 = (s32[128]{0:T(128)}, s32[128]{0:T(128)S(1)}, u32[]{:S(2)}) copy-start(s32[128]{0:T(128)S(1)} %multiply_add_fusion.slot) | copy-start | bytes 1540
  3.1 20.0 %all-to-all-start = ((s32[128,1,128]{2,1,0:T(1,128)}), s32[128,1,128]{2,1,0:T(1,128)S(1)}, u32[]{:S(2)}, u32[]{:S(2)}) async-start(s32[128,1,128]{2,1,0:T(1,128)} %bitcast.2), calls=%async_computation | async-start | bytes 131072 | tf_op jit(solution)/shard_map/all_to_all | solution.py:455
  29.6 10.3 %copy-start.9 = (s32[128,1,128]{2,1,0:T(1,128)S(1)}, s32[128,1,128]{2,1,0:T(1,128)}, u32[]{:S(2)}) copy-start(s32[128,1,128]{2,1,0:T(1,128)} %copy-done.8) | copy-start | bytes 196612
  29.6 60.6 %copy-start.10 = (s32[1024]{0:T(1024)S(1)}, s32[1024]{0:T(1024)}, u32[]{:S(2)}) copy-start(s32[1024]{0:T(1024)} %param.9) | copy-start | bytes 12292
  29.6 60.6 %all-to-all-start.1 = ((bf16[256,8,1024]{2,1,0:T(8,128)(2,1)}), bf16[256,8,1024]{2,1,0:T(8,128)(2,1)}, u32[]{:S(2)}, u32[]{:S(2)}) async-start(bf16[256,8,1024]{2,1,0:T(8,128)(2,1)} %serve.1), calls=%async_computation.1 | async-start | bytes 8388608 | tf_op jit(solution)/shard_map/all_to_all | solution.py:455
  102.8 10.9 %copy-start.17 = (bf16[128,1024]{1,0:T(8,128)(2,1)S(1)}, bf16[128,1024]{1,0:T(8,128)(2,1)}, u32[]{:S(2)}) copy-start(bf16[128,1024]{1,0:T(8,128)(2,1)} %get-tuple-element.47) | copy-start | bytes 786436
  102.8 13.3 %copy-start.16 = (bf16[128,1024]{1,0:T(8,128)(2,1)S(1)}, bf16[128,1024]{1,0:T(8,128)(2,1)}, u32[]{:S(2)}) copy-start(bf16[128,1024]{1,0:T(8,128)(2,1)} %get-tuple-element.48) | copy-start | bytes 786436
  102.8 15.8 %copy-start.15 = (bf16[128,1024]{1,0:T(8,128)(2,1)S(1)}, bf16[128,1024]{1,0:T(8,128)(2,1)}, u32[]{:S(2)}) copy-start(bf16[128,1024]{1,0:T(8,128)(2,1)} %get-tuple-element.49) | copy-start | bytes 786436
  102.8 74.8 %copy-start.14 = (bf16[128,1024]{1,0:T(8,128)(2,1)S(1)}, bf16[128,1024]{1,0:T(8,128)(2,1)}, u32[]{:S(2)}) copy-start(bf16[128,1024]{1,0:T(8,128)(2,1)} %get-tuple-element.39) | copy-start | bytes 786436
  102.8 79.3 %copy-start.13 = (bf16[128,1024]{1,0:T(8,128)(2,1)S(1)}, bf16[128,1024]{1,0:T(8,128)(2,1)}, u32[]{:S(2)}) copy-start(bf16[128,1024]{1,0:T(8,128)(2,1)} %get-tuple-element.40) | copy-start | bytes 786436
  102.8 80.1 %copy-start.12 = (bf16[128,1024]{1,0:T(8,128)(2,1)S(1)}, bf16[128,1024]{1,0:T(8,128)(2,1)}, u32[]{:S(2)}) copy-start(bf16[128,1024]{1,0:T(8,128)(2,1)} %get-tuple-element.41) | copy-start | bytes 786436
  102.8 81.6 %all-to-all-start.2 = ((bf16[128,8,2432]{2,1,0:T(8,128)(2,1)}), bf16[128,8,2432]{2,1,0:T(8,128)(2,1)}, u32[]{:S(2)}, u32[]{:S(2)}) async-start(bf16[128,8,2432]{2,1,0:T(8,128)(2,1)} %weigh.1), calls=%async_computation.2 | async-start | bytes 9961472 | tf_op jit(solution)/shard_map/all_to_all | solution.py:455
  109.8 62.8 %collective-permute-start = (bf16[128,1024]{1,0:T(8,128)(2,1)S(1)}, bf16[128,1024]{1,0:T(8,128)(2,1)S(1)}, u32[]{:S(2)}, u32[]{:S(2)}) collective-permute-start(bf16[128,1024]{1,0:T(8,128)(2,1)S(1)} %copy-done.19), channel_id=1, source_target_pairs={{0,1},{1,2},{2,3},{3,4},{4,5},{5,6},{6,7},{7,8},{8,9},{9,10},{10,1... | collective-permute-start | bytes 786440 | tf_op jit(solution)/shard_map/ppermute | solution.py:479
  111.2 66.4 %collective-permute-start.1 = (bf16[128,1024]{1,0:T(8,128)(2,1)S(1)}, bf16[128,1024]{1,0:T(8,128)(2,1)S(1)}, u32[]{:S(2)}, u32[]{:S(2)}) collective-permute-start(bf16[128,1024]{1,0:T(8,128)(2,1)S(1)} %copy-done.18), channel_id=1, source_target_pairs={{0,2},{1,3},{2,4},{3,5},{4,6},{5,7},{6,8},{7,9},{8,10},{9,11},{10,... | collective-permute-start | bytes 786440 | tf_op jit(solution)/shard_map/ppermute | solution.py:479
  113.7 63.9 %collective-permute-start.10 = (bf16[128,1024]{1,0:T(8,128)(2,1)S(1)}, bf16[128,1024]{1,0:T(8,128)(2,1)S(1)}, u32[]{:S(2)}, u32[]{:S(2)}) collective-permute-start(bf16[128,1024]{1,0:T(8,128)(2,1)S(1)} %copy-done.17), channel_id=1, source_target_pairs={{0,11},{1,12},{2,13},{3,14},{4,15},{5,0},{6,1},{7,2},{8,3},{9,4},{... | collective-permute-start | bytes 786440 | tf_op jit(solution)/shard_map/ppermute | solution.py:479
  116.0 66.1 %collective-permute-start.11 = (bf16[128,1024]{1,0:T(8,128)(2,1)S(1)}, bf16[128,1024]{1,0:T(8,128)(2,1)S(1)}, u32[]{:S(2)}, u32[]{:S(2)}) collective-permute-start(bf16[128,1024]{1,0:T(8,128)(2,1)S(1)} %copy-done.16), channel_id=1, source_target_pairs={{0,12},{1,13},{2,14},{3,15},{4,0},{5,1},{6,2},{7,3},{8,4},{9,5},{1... | collective-permute-start | bytes 786440 | tf_op jit(solution)/shard_map/ppermute | solution.py:479
  118.6 64.2 %collective-permute-start.12 = (bf16[128,1024]{1,0:T(8,128)(2,1)S(1)}, bf16[128,1024]{1,0:T(8,128)(2,1)S(1)}, u32[]{:S(2)}, u32[]{:S(2)}) collective-permute-start(bf16[128,1024]{1,0:T(8,128)(2,1)S(1)} %copy-done.15), channel_id=1, source_target_pairs={{0,13},{1,14},{2,15},{3,0},{4,1},{5,2},{6,3},{7,4},{8,5},{9,6},{10... | collective-permute-start | bytes 786440 | tf_op jit(solution)/shard_map/ppermute | solution.py:479
  172.7 33.6 %collective-permute-start.13 = (bf16[128,1024]{1,0:T(8,128)(2,1)}, bf16[128,1024]{1,0:T(8,128)(2,1)S(1)}, u32[]{:S(2)}, u32[]{:S(2)}) collective-permute-start(bf16[128,1024]{1,0:T(8,128)(2,1)} %get-tuple-element.50), channel_id=1, source_target_pairs={{0,14},{1,15},{2,0},{3,1},{4,2},{5,3},{6,4},{7,5},{8,6},{9,7},{10,... | collective-permute-start | bytes 786440 | tf_op jit(solution)/shard_map/ppermute | solution.py:479
  177.5 32.8 %collective-permute-start.14 = (bf16[128,1024]{1,0:T(8,128)(2,1)}, bf16[128,1024]{1,0:T(8,128)(2,1)S(1)}, u32[]{:S(2)}, u32[]{:S(2)}) collective-permute-start(bf16[128,1024]{1,0:T(8,128)(2,1)} %get-tuple-element.51), channel_id=1, source_target_pairs={{0,15},{1,0},{2,1},{3,2},{4,3},{5,4},{6,5},{7,6},{8,7},{9,8},{10,9... | collective-permute-start | bytes 786440 | tf_op jit(solution)/shard_map/ppermute | solution.py:479
  177.6 33.1 %collective-permute-start.2 = (bf16[128,1024]{1,0:T(8,128)(2,1)S(1)}, bf16[128,1024]{1,0:T(8,128)(2,1)S(1)}, u32[]{:S(2)}, u32[]{:S(2)}) collective-permute-start(bf16[128,1024]{1,0:T(8,128)(2,1)S(1)} %copy-done.14), channel_id=1, source_target_pairs={{0,3},{1,4},{2,5},{3,6},{4,7},{5,8},{6,9},{7,10},{8,11},{9,12},{10... | collective-permute-start | bytes 786440 | tf_op jit(solution)/shard_map/ppermute | solution.py:479
  182.1 32.3 %collective-permute-start.3 = (bf16[128,1024]{1,0:T(8,128)(2,1)S(1)}, bf16[128,1024]{1,0:T(8,128)(2,1)S(1)}, u32[]{:S(2)}, u32[]{:S(2)}) collective-permute-start(bf16[128,1024]{1,0:T(8,128)(2,1)S(1)} %copy-done.13), channel_id=1, source_target_pairs={{0,4},{1,5},{2,6},{3,7},{4,8},{5,9},{6,10},{7,11},{8,12},{9,13},{1... | collective-permute-start | bytes 786440 | tf_op jit(solution)/shard_map/ppermute | solution.py:479
  182.9 32.4 %collective-permute-start.4 = (bf16[128,1024]{1,0:T(8,128)(2,1)S(1)}, bf16[128,1024]{1,0:T(8,128)(2,1)S(1)}, u32[]{:S(2)}, u32[]{:S(2)}) collective-permute-start(bf16[128,1024]{1,0:T(8,128)(2,1)S(1)} %copy-done.12), channel_id=1, source_target_pairs={{0,5},{1,6},{2,7},{3,8},{4,9},{5,10},{6,11},{7,12},{8,13},{9,14},{... | collective-permute-start | bytes 786440 | tf_op jit(solution)/shard_map/ppermute | solution.py:479
  187.3 66.6 %all-to-all-start.3 = ((bf16[128,8,256]{2,1,0:T(8,128)(2,1)}), bf16[128,8,256]{2,1,0:T(8,128)(2,1)}, u32[]{:S(2)}, u32[]{:S(2)}) async-start(bf16[128,8,256]{2,1,0:T(8,128)(2,1)} %get-tuple-element.52), calls=%async_computation.3 | async-start | bytes 1048576 | tf_op jit(solution)/shard_map/all_to_all | solution.py:455
  206.3 24.2 %collective-permute-start.5 = (bf16[128,1024]{1,0:T(8,128)(2,1)}, bf16[128,1024]{1,0:T(8,128)(2,1)}, u32[]{:S(2)}, u32[]{:S(2)}) collective-permute-start(bf16[128,1024]{1,0:T(8,128)(2,1)} %get-tuple-element.42), channel_id=1, source_target_pairs={{0,6},{1,7},{2,8},{3,9},{4,10},{5,11},{6,12},{7,13},{8,14},{9,15},... | collective-permute-start | bytes 786440 | tf_op jit(solution)/shard_map/ppermute | solution.py:479
  210.3 24.9 %collective-permute-start.6 = (bf16[128,1024]{1,0:T(8,128)(2,1)}, bf16[128,1024]{1,0:T(8,128)(2,1)}, u32[]{:S(2)}, u32[]{:S(2)}) collective-permute-start(bf16[128,1024]{1,0:T(8,128)(2,1)} %get-tuple-element.43), channel_id=1, source_target_pairs={{0,7},{1,8},{2,9},{3,10},{4,11},{5,12},{6,13},{7,14},{8,15},{9,0},... | collective-permute-start | bytes 786440 | tf_op jit(solution)/shard_map/ppermute | solution.py:479
  210.7 35.2 %collective-permute-start.7 = (bf16[128,1024]{1,0:T(8,128)(2,1)}, bf16[128,1024]{1,0:T(8,128)(2,1)}, u32[]{:S(2)}, u32[]{:S(2)}) collective-permute-start(bf16[128,1024]{1,0:T(8,128)(2,1)} %get-tuple-element.44), channel_id=1, source_target_pairs={{0,8},{1,9},{2,10},{3,11},{4,12},{5,13},{6,14},{7,15},{8,0},{9,1},... | collective-permute-start | bytes 786440 | tf_op jit(solution)/shard_map/ppermute | solution.py:479
  215.1 30.7 %collective-permute-start.8 = (bf16[128,1024]{1,0:T(8,128)(2,1)}, bf16[128,1024]{1,0:T(8,128)(2,1)}, u32[]{:S(2)}, u32[]{:S(2)}) collective-permute-start(bf16[128,1024]{1,0:T(8,128)(2,1)} %get-tuple-element.45), channel_id=1, source_target_pairs={{0,9},{1,10},{2,11},{3,12},{4,13},{5,14},{6,15},{7,0},{8,1},{9,2},... | collective-permute-start | bytes 786440 | tf_op jit(solution)/shard_map/ppermute | solution.py:479
  216.0 29.9 %copy-start = (bf16[1,512,1024]{2,1,0:T(8,128)(2,1)S(1)}, bf16[1,512,1024]{2,1,0:T(8,128)(2,1)}, u32[]{:S(2)}) copy-start(bf16[1,512,1024]{2,1,0:T(8,128)(2,1)} %param.14) | copy-start | bytes 3145732
  216.0 29.9 %copy-start.1 = (bf16[128,1024]{1,0:T(8,128)(2,1)S(1)}, bf16[128,1024]{1,0:T(8,128)(2,1)}, u32[]{:S(2)}) copy-start(bf16[128,1024]{1,0:T(8,128)(2,1)} %get-tuple-element.36.refs_0_) | copy-start | bytes 786436
  216.0 29.9 %copy-start.6 = (bf16[16,8,128]{2,1,0:T(8,128)(2,1)S(1)}, bf16[16,8,128]{2,1,0:T(8,128)(2,1)}, u32[]{:S(2)}) copy-start(bf16[16,8,128]{2,1,0:T(8,128)(2,1)} %get-tuple-element.35.ext_ref) | copy-start | bytes 98308
  216.0 29.9 %copy-start.7 = (s32[5]{0:T(128)S(1)}, s32[5]{0:T(128)}, u32[]{:S(2)}) copy-start(s32[5]{0:T(128)} %stack.23.place) | copy-start | bytes 64
  216.0 29.9 %collective-permute-start.9 = (bf16[128,1024]{1,0:T(8,128)(2,1)}, bf16[128,1024]{1,0:T(8,128)(2,1)}, u32[]{:S(2)}, u32[]{:S(2)}) collective-permute-start(bf16[128,1024]{1,0:T(8,128)(2,1)} %get-tuple-element.46), channel_id=1, source_target_pairs={{0,10},{1,11},{2,12},{3,13},{4,14},{5,15},{6,0},{7,1},{8,2},{9,3},... | collective-permute-start | bytes 786440 | tf_op jit(solution)/shard_map/ppermute | solution.py:479
  (7 other events, 19.4 us)
